TPU v7x, 256 devices: a whole 4x4x8 slice. The times are simulated.
256 devices in a mesh: cls: 16 (over y, x), batch: 16 (over z, core).
Axes of the slice: x: 4, y: 4, z: 8, core: 2. Of those that a mesh axis runs over, the one named last changes fastest.
Arguments:
- particles: bfloat16 [2048, 5120, 128], P('batch', 'cls'), may hold values from -6 to 6
- volumes: bfloat16 [16, 5120, 128], P('batch', 'cls'), may hold values from -6 to 6
- assignment: int32 [2048], P('batch'), may hold values from 0 to 15
- defocus: float32 [2048], P('batch'), may hold values from 1 to 8
- tilt_limits: int32 [2048, 2], P('batch'), may hold values from 2 to 16
- orientation: int32 [2048], P('batch'), may hold values from 0 to 7
Outputs:
- updated: float32 [16, 5120, 128], P('batch', 'cls')
- scores: float32 [2048], P('batch')
All inputs are finite; a program needn't handle non-finite values.
Results may differ from a plain program's by a relative error of at most 0.0015.
Values may be sent and summed in bfloat16 or wider, within the bound.
A program may use at most 128 MiB of HBM per device.

v0:
```python
import math

import jax
import jax.numpy as jnp
from jax import lax
from jax.sharding import PartitionSpec as P

ORIENTS = 8


step_size = 0.5
phase_offset = 0.1


def make_tables(line_length):
    index = jnp.arange(line_length, dtype=jnp.int32)
    angle = (
        2.0
        * math.pi
        * (index[:, None] * index[None, :] % line_length).astype(jnp.float32)
        / line_length
    )
    cosine = jnp.cos(angle)
    sine = jnp.sin(angle)
    forward_model = jnp.concatenate([cosine, -sine], axis=1).astype(jnp.bfloat16)
    back = jnp.concatenate([cosine, -sine], axis=0) / line_length
    return (forward_model, back)


def make_filters(defocus, tilt_limits, orientation, radius, line_length, orients):
    freq = jnp.arange(line_length, dtype=jnp.int32)
    signed = jnp.where(freq < line_length // 2, freq, freq - line_length)
    half = line_length // 2
    along_s = (
        math.pi
        * defocus[:, None]
        * ((signed * signed).astype(jnp.float32) / float(half * half))[None, :]
        + phase_offset
    )
    along_r = (
        math.pi
        * defocus[:, None]
        * ((radius * radius).astype(jnp.float32) / float(half * half))[None, :]
    )
    ctf = -(
        jnp.sin(along_s)[:, None, :] * jnp.cos(along_r)[:, :, None]
        + jnp.cos(along_s)[:, None, :] * jnp.sin(along_r)[:, :, None]
    )
    plus = tilt_limits[:, 0][:, None, None]
    minus = tilt_limits[:, 1][:, None, None]
    sgrid = signed[None, None, :]
    rgrid = radius[None, :, None]
    keep = jnp.where(sgrid >= 0, 8 * sgrid <= plus * rgrid, -8 * sgrid <= minus * rgrid)
    amp = ctf * keep.astype(jnp.float32)
    shift = orientation * (line_length // orients)
    turn = (
        2.0
        * math.pi
        * (freq[None, :] * shift[:, None] % line_length).astype(jnp.float32)
        / line_length
    )
    filtered_real = amp * jnp.cos(turn)[:, None, :]
    filtered_imaginary = -amp * jnp.sin(turn)[:, None, :]
    return (filtered_real, filtered_imaginary)


def transform(samples, forward_model):
    number, line_rows, line_length = samples.shape
    result = jnp.dot(
        samples.reshape(number * line_rows, line_length),
        forward_model,
        preferred_element_type=jnp.float32,
    )
    return result.astype(jnp.bfloat16).reshape(number, line_rows, 2 * line_length)


def invert(spectra, back):
    number, line_rows, width = spectra.shape
    result = jnp.dot(
        spectra.reshape(number * line_rows, width),
        back,
        precision=lax.Precision.HIGHEST,
        preferred_element_type=jnp.float32,
    )
    return result.reshape(number, line_rows, width // 2)


def local(particles, volumes, assignment, defocus, tilt_limits, orientation):
    line_length = particles.shape[2]
    line_rows = particles.shape[1]
    total = particles.shape[0]
    forward_model, back = make_tables(line_length)
    classes = volumes.shape[0] * lax.axis_size("batch")
    spectra = lax.all_gather(transform(volumes, forward_model), "batch", axis=0, tiled=True)
    flat_spectra = spectra.reshape(classes, line_rows * 2 * line_length)
    first_line = lax.axis_index("cls") * line_rows
    radius = 1 + (first_line + jnp.arange(line_rows, dtype=jnp.int32)) % (line_length // 2)
    scale = 1.0 / (line_rows * lax.axis_size("cls") * line_length * line_length)
    block_range = min(total, 32)
    count = total // block_range
    class_ids = jnp.arange(classes, dtype=jnp.int32)

    def step(carry, items):
        sums, counts = carry
        group_spectra, group_a, group_d, group_t, group_o = items
        spectrum_estimate = jnp.dot(
            group_spectra.reshape(block_range * line_rows, line_length),
            forward_model,
            preferred_element_type=jnp.float32,
        )
        spectrum_estimate = spectrum_estimate.reshape(block_range, line_rows, 2 * line_length)
        onehot = group_a[:, None] == class_ids[None, :]
        chosen_class = jnp.dot(
            onehot.astype(jnp.bfloat16), flat_spectra, preferred_element_type=jnp.float32
        )
        chosen_class = chosen_class.reshape(block_range, line_rows, 2 * line_length)
        filtered_real, filtered_imaginary = make_filters(
            group_d, group_t, group_o, radius, line_length, ORIENTS
        )
        volume_real = chosen_class[:, :, :line_length]
        volume_imaginary = chosen_class[:, :, line_length:]
        residual_real = spectrum_estimate[:, :, :line_length] - (
            filtered_real * volume_real - filtered_imaginary * volume_imaginary
        )
        residual_imaginary = spectrum_estimate[:, :, line_length:] - (
            filtered_real * volume_imaginary + filtered_imaginary * volume_real
        )
        score = (
            jnp.sum(
                residual_real * residual_real + residual_imaginary * residual_imaginary, axis=(1, 2)
            )
            * scale
        )
        grads = jnp.concatenate(
            [
                filtered_real * residual_real + filtered_imaginary * residual_imaginary,
                filtered_real * residual_imaginary - filtered_imaginary * residual_real,
            ],
            axis=2,
        )
        weights = onehot.astype(jnp.float32)
        sums = sums + jnp.dot(
            weights.T,
            grads.reshape(block_range, line_rows * 2 * line_length),
            precision=lax.Precision.HIGHEST,
            preferred_element_type=jnp.float32,
        )
        counts = counts + jnp.sum(weights, axis=0)
        return ((sums, counts), score)

    items = (
        particles.reshape(count, block_range, line_rows, line_length),
        assignment.reshape(count, block_range),
        defocus.reshape(count, block_range),
        tilt_limits.reshape(count, block_range, 2),
        orientation.reshape(count, block_range),
    )
    start = (
        jnp.zeros((classes, line_rows * 2 * line_length), jnp.float32),
        jnp.zeros((classes,), jnp.float32),
    )
    (sums, counts), partial_scores = lax.scan(step, start, items)
    scores = lax.psum(partial_scores.reshape(total), "cls")
    sums = sums.reshape(classes, line_rows, 2 * line_length)
    owned, owned_counts = (
        lax.psum_scatter(
            sums.astype(jnp.bfloat16), "batch", scatter_dimension=0, tiled=True
        ).astype(jnp.float32),
        lax.psum_scatter(
            counts.astype(jnp.bfloat16), "batch", scatter_dimension=0, tiled=True
        ).astype(jnp.float32),
    )
    grad = invert(owned, back)
    updated = volumes.astype(jnp.float32) + step_size * grad / (owned_counts + 1.0)[:, None, None]
    return (updated, scores)


def solution(mesh):
    in_specs = (
        P("batch", "cls", None),
        P("batch", "cls", None),
        P("batch"),
        P("batch"),
        P("batch", None),
        P("batch"),
    )
    out_specs = (P("batch", "cls", None), P("batch"))
    return jax.shard_map(local, mesh=mesh, in_specs=in_specs, out_specs=out_specs, check_vma=False)
```

profile of v0, /device:TPU:1, one launch (start us, length us, event | category | flops | bytes accessed | tf_op | source)
XLA Modules:
  0.0 367.4 jit_solution(17279591881168893671)
XLA Ops:
  7.2 0.3 fusion.57
  7.5 1.7 fusion.41
  9.3 0.8 reshape.401
  10.1 0.7 reshape.400
  10.8 0.7 reshape.402
  11.6 0.7 reshape.403
  12.3 42.3 %all-gather.3.cloned.1.call-done = bf16[5120,256]{1,0:T(8,128)(2,1)} async-done(((bf16[320,256]{1,0:T(8,128)(2,1)}), bf16[5120,256]{1,0:T(8,128)(2,1)}) %all-gather.3.cloned.1.call-update) | async-done | bytes 2621456 | tf_op jit(solution)/shard_map/all_gather | solution.py:94
  54.7 2.5 reshape.407
  57.2 236.4 %while.19 = (s32[]{:T(128)}, f32[16,81920]{1,0:T(8,128)}, f32[16]{0:T(128)S(1)}, f32[4,32]{1,0:T(4,128)S(1)}, s32[4,32]{1,0:T(4,128)S(1)}, /*index=5*/s32[4,32,2...) while((s32[]{:T(128)}, f32[16,81920]{1,0:T(8,128)}, ...), condition=%wide.region_3.4_spmd.clone.clone.clone, body=%wide.region_0.3_spmd.clone.clone.clone.sunk | while | flops 1316072960 | bytes 163296944 | solution.py:162
  57.4 4.8 %fusion.82 = f32[32,81920]{1,0:T(8,128)} fusion(bf16[16,81920]{1,0:T(8,128)(2,1)S(1)} %get-tuple-element.520, s32[32]{0:T(128)S(1)} %get-tuple-element.463), kind=kOutput, calls=%fused_computation.36.clone.1 | convolution fusion | flops 83886592 | bytes 13107328 | tf_op jit(solution)/shard_map/while/body/eval_jaxpr/dot_general | solution.py:113
  62.2 7.2 %copy.17 = f32[4,8,320,256]{3,2,1,0:T(8,128)S(1)} copy(f32[4,8,320,256]{3,1,2,0:T(8,128)} %bitcast.74) | data formatting | bytes 20971520 | tf_op jit(solution)/shard_map/while
  69.5 0.3 multiply_cosine_fusion.2
  69.7 0.2 fusion.83
  69.9 0.1 fusion.86
  70.0 3.3 fusion.88
  73.3 8.9 %add_reduce_fusion.2 = (f32[32]{0:T(128)S(1)}, f32[32,320,128]{2,1,0:T(8,128)S(1)}, f32[32,320,128]{2,1,0:T(8,128)}) fusion(f32[32,320,256]{2,1,0:T(8,128)S(1)} %bitcast.72, f32[32,128]{1,0:T(8,128)S(1)} %get-tuple-element.465, f32[32,128]{1,0:T(8,128)S(1)} %get-tuple-element.466, f32[32,320]{1,0:T(8,128)S(1)} %get-tuple-element.467, ...), kind=kLoop, calls=%fused_computation.7.clone.1 | loop fusion | flops 30146528 | bytes 31687936 | tf_op jit(solution)/shard_map/while/body/eval_jaxpr/reduce_sum | solution.py:129
  82.3 8.9 %multiply_add_fusion.3 = (f32[32,320,128]{2,1,0:T(8,128)}, f32[32,320,128]{2,1,0:T(8,128)}) fusion(f32[32,320,128]{2,1,0:T(8,128)S(1)} %get-tuple-element.477, f32[32,320,128]{2,1,0:T(8,128)} %get-tuple-element.478, f32[32,128]{1,0:T(8,128)S(1)} %get-tuple-element.465, f32[32,128]{1,0:T(8,128)S(1)} %get-tuple-element.466, ...), kind=kLoop, calls=%fused_computation.9.clone.1 | loop fusion | flops 22282240 | bytes 21202048 | tf_op jit(solution)/shard_map/while/body/eval_jaxpr/add | solution.py:136
  91.2 4.9 %pad_maximum_fusion.4 = f32[32,320,256]{2,1,0:T(8,128)S(1)} fusion(f32[32,320,128]{2,1,0:T(8,128)} %get-tuple-element.479, f32[32,320,128]{2,1,0:T(8,128)} %get-tuple-element.480), kind=kLoop, calls=%fused_computation.4.clone.1 | loop fusion | flops 2621440 | bytes 20971520 | tf_op jit(solution)/shard_map/while/body/eval_jaxpr/concatenate | solution.py:134
  96.1 10.0 %copy.18 = f32[4,8,320,256]{3,1,2,0:T(8,128)} copy(f32[4,8,320,256]{3,2,1,0:T(8,128)S(1)} %bitcast.73) | data formatting | bytes 20971520 | tf_op jit(solution)/shard_map/while
  106.1 9.3 %convolution_add_fusion.2 = f32[16,81920]{1,0:T(8,128)} fusion(f32[32,81920]{1,0:T(8,128)} %bitcast.75, f32[16,81920]{1,0:T(8,128)} %get-tuple-element.497, pred[]{:T(512)S(6)} %compare.14, s32[32]{0:T(128)S(1)} %get-tuple-element.463), kind=kOutput, calls=%fused_computation.3.clone.1 | convolution fusion | flops 505938432 | bytes 20971648 | tf_op jit(solution)/shard_map/while/body/eval_jaxpr/dot_general | solution.py:142
  115.4 0.1 fusion.89
  115.7 4.8 %fusion.82 = f32[32,81920]{1,0:T(8,128)} fusion(bf16[16,81920]{1,0:T(8,128)(2,1)S(1)} %get-tuple-element.520, s32[32]{0:T(128)S(1)} %get-tuple-element.463), kind=kOutput, calls=%fused_computation.36.clone.1 | convolution fusion | flops 83886592 | bytes 13107328 | tf_op jit(solution)/shard_map/while/body/eval_jaxpr/dot_general | solution.py:113
  120.5 7.2 %copy.17 = f32[4,8,320,256]{3,2,1,0:T(8,128)S(1)} copy(f32[4,8,320,256]{3,1,2,0:T(8,128)} %bitcast.74) | data formatting | bytes 20971520 | tf_op jit(solution)/shard_map/while
  127.8 0.3 multiply_cosine_fusion.2
  128.0 0.2 fusion.83
  128.2 0.1 fusion.86
  128.3 3.2 fusion.88
  131.6 8.9 %add_reduce_fusion.2 = (f32[32]{0:T(128)S(1)}, f32[32,320,128]{2,1,0:T(8,128)S(1)}, f32[32,320,128]{2,1,0:T(8,128)}) fusion(f32[32,320,256]{2,1,0:T(8,128)S(1)} %bitcast.72, f32[32,128]{1,0:T(8,128)S(1)} %get-tuple-element.465, f32[32,128]{1,0:T(8,128)S(1)} %get-tuple-element.466, f32[32,320]{1,0:T(8,128)S(1)} %get-tuple-element.467, ...), kind=kLoop, calls=%fused_computation.7.clone.1 | loop fusion | flops 30146528 | bytes 31687936 | tf_op jit(solution)/shard_map/while/body/eval_jaxpr/reduce_sum | solution.py:129
  140.6 8.9 %multiply_add_fusion.3 = (f32[32,320,128]{2,1,0:T(8,128)}, f32[32,320,128]{2,1,0:T(8,128)}) fusion(f32[32,320,128]{2,1,0:T(8,128)S(1)} %get-tuple-element.477, f32[32,320,128]{2,1,0:T(8,128)} %get-tuple-element.478, f32[32,128]{1,0:T(8,128)S(1)} %get-tuple-element.465, f32[32,128]{1,0:T(8,128)S(1)} %get-tuple-element.466, ...), kind=kLoop, calls=%fused_computation.9.clone.1 | loop fusion | flops 22282240 | bytes 21202048 | tf_op jit(solution)/shard_map/while/body/eval_jaxpr/add | solution.py:136
  149.5 4.9 %pad_maximum_fusion.4 = f32[32,320,256]{2,1,0:T(8,128)S(1)} fusion(f32[32,320,128]{2,1,0:T(8,128)} %get-tuple-element.479, f32[32,320,128]{2,1,0:T(8,128)} %get-tuple-element.480), kind=kLoop, calls=%fused_computation.4.clone.1 | loop fusion | flops 2621440 | bytes 20971520 | tf_op jit(solution)/shard_map/while/body/eval_jaxpr/concatenate | solution.py:134
  154.4 10.0 %copy.18 = f32[4,8,320,256]{3,1,2,0:T(8,128)} copy(f32[4,8,320,256]{3,2,1,0:T(8,128)S(1)} %bitcast.73) | data formatting | bytes 20971520 | tf_op jit(solution)/shard_map/while
  164.4 10.3 %convolution_add_fusion.2 = f32[16,81920]{1,0:T(8,128)} fusion(f32[32,81920]{1,0:T(8,128)} %bitcast.75, f32[16,81920]{1,0:T(8,128)} %get-tuple-element.497, pred[]{:T(512)S(6)} %compare.14, s32[32]{0:T(128)S(1)} %get-tuple-element.463), kind=kOutput, calls=%fused_computation.3.clone.1 | convolution fusion | flops 505938432 | bytes 20971648 | tf_op jit(solution)/shard_map/while/body/eval_jaxpr/dot_general | solution.py:142
  174.8 0.1 fusion.89
  175.1 4.8 %fusion.82 = f32[32,81920]{1,0:T(8,128)} fusion(bf16[16,81920]{1,0:T(8,128)(2,1)S(1)} %get-tuple-element.520, s32[32]{0:T(128)S(1)} %get-tuple-element.463), kind=kOutput, calls=%fused_computation.36.clone.1 | convolution fusion | flops 83886592 | bytes 13107328 | tf_op jit(solution)/shard_map/while/body/eval_jaxpr/dot_general | solution.py:113
  179.9 7.2 %copy.17 = f32[4,8,320,256]{3,2,1,0:T(8,128)S(1)} copy(f32[4,8,320,256]{3,1,2,0:T(8,128)} %bitcast.74) | data formatting | bytes 20971520 | tf_op jit(solution)/shard_map/while
  187.1 0.3 multiply_cosine_fusion.2
  187.4 0.2 fusion.83
  187.6 0.1 fusion.86
  187.7 3.2 fusion.88
  191.0 8.9 %add_reduce_fusion.2 = (f32[32]{0:T(128)S(1)}, f32[32,320,128]{2,1,0:T(8,128)S(1)}, f32[32,320,128]{2,1,0:T(8,128)}) fusion(f32[32,320,256]{2,1,0:T(8,128)S(1)} %bitcast.72, f32[32,128]{1,0:T(8,128)S(1)} %get-tuple-element.465, f32[32,128]{1,0:T(8,128)S(1)} %get-tuple-element.466, f32[32,320]{1,0:T(8,128)S(1)} %get-tuple-element.467, ...), kind=kLoop, calls=%fused_computation.7.clone.1 | loop fusion | flops 30146528 | bytes 31687936 | tf_op jit(solution)/shard_map/while/body/eval_jaxpr/reduce_sum | solution.py:129
  199.9 8.9 %multiply_add_fusion.3 = (f32[32,320,128]{2,1,0:T(8,128)}, f32[32,320,128]{2,1,0:T(8,128)}) fusion(f32[32,320,128]{2,1,0:T(8,128)S(1)} %get-tuple-element.477, f32[32,320,128]{2,1,0:T(8,128)} %get-tuple-element.478, f32[32,128]{1,0:T(8,128)S(1)} %get-tuple-element.465, f32[32,128]{1,0:T(8,128)S(1)} %get-tuple-element.466, ...), kind=kLoop, calls=%fused_computation.9.clone.1 | loop fusion | flops 22282240 | bytes 21202048 | tf_op jit(solution)/shard_map/while/body/eval_jaxpr/add | solution.py:136
  208.9 4.9 %pad_maximum_fusion.4 = f32[32,320,256]{2,1,0:T(8,128)S(1)} fusion(f32[32,320,128]{2,1,0:T(8,128)} %get-tuple-element.479, f32[32,320,128]{2,1,0:T(8,128)} %get-tuple-element.480), kind=kLoop, calls=%fused_computation.4.clone.1 | loop fusion | flops 2621440 | bytes 20971520 | tf_op jit(solution)/shard_map/while/body/eval_jaxpr/concatenate | solution.py:134
  213.8 10.0 %copy.18 = f32[4,8,320,256]{3,1,2,0:T(8,128)} copy(f32[4,8,320,256]{3,2,1,0:T(8,128)S(1)} %bitcast.73) | data formatting | bytes 20971520 | tf_op jit(solution)/shard_map/while
  223.8 10.3 %convolution_add_fusion.2 = f32[16,81920]{1,0:T(8,128)} fusion(f32[32,81920]{1,0:T(8,128)} %bitcast.75, f32[16,81920]{1,0:T(8,128)} %get-tuple-element.497, pred[]{:T(512)S(6)} %compare.14, s32[32]{0:T(128)S(1)} %get-tuple-element.463), kind=kOutput, calls=%fused_computation.3.clone.1 | convolution fusion | flops 505938432 | bytes 20971648 | tf_op jit(solution)/shard_map/while/body/eval_jaxpr/dot_general | solution.py:142
  234.2 0.1 fusion.89
  234.4 4.8 %fusion.82 = f32[32,81920]{1,0:T(8,128)} fusion(bf16[16,81920]{1,0:T(8,128)(2,1)S(1)} %get-tuple-element.520, s32[32]{0:T(128)S(1)} %get-tuple-element.463), kind=kOutput, calls=%fused_computation.36.clone.1 | convolution fusion | flops 83886592 | bytes 13107328 | tf_op jit(solution)/shard_map/while/body/eval_jaxpr/dot_general | solution.py:113
  239.3 7.2 %copy.17 = f32[4,8,320,256]{3,2,1,0:T(8,128)S(1)} copy(f32[4,8,320,256]{3,1,2,0:T(8,128)} %bitcast.74) | data formatting | bytes 20971520 | tf_op jit(solution)/shard_map/while
  246.5 0.3 multiply_cosine_fusion.2
  246.8 0.2 fusion.83
  246.9 0.1 fusion.86
  247.1 3.2 fusion.88
  250.4 8.9 %add_reduce_fusion.2 = (f32[32]{0:T(128)S(1)}, f32[32,320,128]{2,1,0:T(8,128)S(1)}, f32[32,320,128]{2,1,0:T(8,128)}) fusion(f32[32,320,256]{2,1,0:T(8,128)S(1)} %bitcast.72, f32[32,128]{1,0:T(8,128)S(1)} %get-tuple-element.465, f32[32,128]{1,0:T(8,128)S(1)} %get-tuple-element.466, f32[32,320]{1,0:T(8,128)S(1)} %get-tuple-element.467, ...), kind=kLoop, calls=%fused_computation.7.clone.1 | loop fusion | flops 30146528 | bytes 31687936 | tf_op jit(solution)/shard_map/while/body/eval_jaxpr/reduce_sum | solution.py:129
  259.3 8.9 %multiply_add_fusion.3 = (f32[32,320,128]{2,1,0:T(8,128)}, f32[32,320,128]{2,1,0:T(8,128)}) fusion(f32[32,320,128]{2,1,0:T(8,128)S(1)} %get-tuple-element.477, f32[32,320,128]{2,1,0:T(8,128)} %get-tuple-element.478, f32[32,128]{1,0:T(8,128)S(1)} %get-tuple-element.465, f32[32,128]{1,0:T(8,128)S(1)} %get-tuple-element.466, ...), kind=kLoop, calls=%fused_computation.9.clone.1 | loop fusion | flops 22282240 | bytes 21202048 | tf_op jit(solution)/shard_map/while/body/eval_jaxpr/add | solution.py:136
  268.3 4.9 %pad_maximum_fusion.4 = f32[32,320,256]{2,1,0:T(8,128)S(1)} fusion(f32[32,320,128]{2,1,0:T(8,128)} %get-tuple-element.479, f32[32,320,128]{2,1,0:T(8,128)} %get-tuple-element.480), kind=kLoop, calls=%fused_computation.4.clone.1 | loop fusion | flops 2621440 | bytes 20971520 | tf_op jit(solution)/shard_map/while/body/eval_jaxpr/concatenate | solution.py:134
  273.1 10.0 %copy.18 = f32[4,8,320,256]{3,1,2,0:T(8,128)} copy(f32[4,8,320,256]{3,2,1,0:T(8,128)S(1)} %bitcast.73) | data formatting | bytes 20971520 | tf_op jit(solution)/shard_map/while
  283.2 10.3 %convolution_add_fusion.2 = f32[16,81920]{1,0:T(8,128)} fusion(f32[32,81920]{1,0:T(8,128)} %bitcast.75, f32[16,81920]{1,0:T(8,128)} %get-tuple-element.497, pred[]{:T(512)S(6)} %compare.14, s32[32]{0:T(128)S(1)} %get-tuple-element.463), kind=kOutput, calls=%fused_computation.3.clone.1 | convolution fusion | flops 505938432 | bytes 20971648 | tf_op jit(solution)/shard_map/while/body/eval_jaxpr/dot_general | solution.py:142
  293.7 2.7 convert_element_type.83
  296.4 2.1 copy.14
  298.6 0.3 sine_negate_fusion
  298.9 0.6 dynamic-slice
  299.5 23.2 %all-reduce = bf16[16]{0:T(256)(128)(2,1)S(1)} all-reduce(bf16[16]{0:T(256)(128)(2,1)S(1)} %convert_element_type.85), channel_id=4, replica_groups=mesh['cls'=16,'batch'=16] {'batch'}, use_global_device_ids=true, to_apply=%region_5.6.clone | all-reduce | flops 16 | bytes 64
  322.7 1.2 dynamic-slice.1
  324.6 34.0 %psum.7 = f32[128]{0:T(128)} all-reduce(f32[128]{0:T(128)S(1)} %reshape.409), channel_id=1, replica_groups=mesh['cls'=16,'batch'=16] {'cls'}, use_global_device_ids=true, to_apply=%region_6.7 | all-reduce | flops 128 | bytes 1024 | tf_op jit(solution)/shard_map/psum | solution.py:163
  358.6 1.9 fusion.44
  (68 shorter events, 1.3 us)
Async XLA Ops:
  7.2 47.5 %all-gather.3.cloned.1.call-start = ((), (), s32[]{:S(2)}) async-start(), calls=%async_computation.2 | async-start | bytes 2785280 | tf_op jit(solution)/shard_map/all_gather | solution.py:94
  9.3 349.4 %reduce-scatter.2.cloned.1.call-start = ((), (), s32[]{:S(2)}) async-start(), calls=%async_computation.1 | async-start | bytes 2785280 | tf_op jit(solution)/shard_map/reduce_scatter | solution.py:166
  296.4 2.4 copy-start.1
  296.4 62.2 %copy-start = (bf16[1,320,128]{2,1,0:T(8,128)(2,1)S(1)}, bf16[1,320,128]{2,1,0:T(8,128)(2,1)}, u32[]{:S(2)}) copy-start(bf16[1,320,128]{2,1,0:T(8,128)(2,1)} %param.9) | copy-start | bytes 245764
Sparse Core Ops, SparseCore 0:
  10.4 44.2 all-gather.2
  298.7 56.4 reduce-scatter.1
where the time goes:
time: 374 us; the launch traced here: 367 us
  other arithmetic  97.7 us (26%)
  local copies, waits for them, and re-layouts  78.6 us (21%)
  matrix products  76.2 us (20%)
  blocking collectives  57.2 us (15%)
  waiting for transfers between devices  42.4 us (11%)
  between operations  14.8 us (4%)
    while x8, local copies, waits for them, and re-layouts  68.9 us
    all_gather x1, waiting for transfers between devices, local(): lax.all_gather(transform(volumes, forward_model), 'batch', axis=0, tiled=...  42.3 us
    dot_general x4, matrix products, step(): jnp.dot(weights.T, grads.reshape(block_range, line_rows * 2 * line_length...  40.2 us
    add x4, other arithmetic, step(): filtered_real * residual_real + filtered_imaginary * residual_imaginary  35.8 us
    reduce_sum x4, other arithmetic, step(): jnp.sum(residual_real * residual_real + residual_imaginary * residual_ima...  35.8 us
    psum x1, blocking collectives, local(): scores = lax.psum(partial_scores.reshape(total), 'cls')  34 us
    unnamed x1, blocking collectives  23.2 us
    concatenate x4, other arithmetic, step(): jnp.concatenate([filtered_real * residual_real + filtered_imaginary * res...  19.5 us
  transfers between devices with their start and end apart: 2, of which 1 were waited for; matrix products, arithmetic and copies ran while one was open for 1% of the time, Pallas kernels for 0%

commit v1 on v0

v1 whole, which is shorter than its diff:
```python
import math

import jax
import jax.numpy as jnp
import numpy as np
from jax import lax
from jax.experimental import pallas as pl
from jax.experimental.pallas import tpu as pltpu
from jax.sharding import PartitionSpec as P

ORIENTS = 8
STEP = 0.5
PHASE = 0.1
BLOCK = 8


def tables(length):
    index = np.arange(length)
    angle = 2.0 * np.pi * ((index[:, None] * index[None, :]) % length) / length
    cosine, sine = np.cos(angle), np.sin(angle)
    forward = np.concatenate([cosine, -sine], axis=1).astype(np.float32)
    back = (np.concatenate([cosine, -sine], axis=0) / length).astype(np.float32)
    turned = jnp.asarray(np.concatenate([forward, forward], axis=0)).astype(jnp.bfloat16)
    back = jnp.asarray(back)
    high = back.astype(jnp.bfloat16)
    low = (back - high.astype(jnp.float32)).astype(jnp.bfloat16)
    return turned, high, low


def amplitudes(defocus, tilt_limits, radius, length):
    freq = jnp.arange(length, dtype=jnp.int32)
    signed = jnp.where(freq < length // 2, freq, freq - length)
    half = length // 2
    along_s = math.pi * defocus[:, None] * ((signed * signed).astype(jnp.float32) / float(half * half))[None, :] + PHASE
    along_r = math.pi * defocus[:, None] * ((radius * radius).astype(jnp.float32) / float(half * half))[None, :]
    ctf = -(
        jnp.sin(along_s)[:, None, :] * jnp.cos(along_r)[:, :, None]
        + jnp.cos(along_s)[:, None, :] * jnp.sin(along_r)[:, :, None]
    )
    limit = jnp.where(signed[None, :] >= 0, tilt_limits[:, 0][:, None], tilt_limits[:, 1][:, None])
    keep = 8 * jnp.abs(signed)[None, None, :] <= limit[:, None, :] * radius[None, :, None]
    return jnp.where(keep, ctf, 0.0)


def main_kernel(cls_ref, ori_ref, x_ref, a_ref, vol_ref, fwd_ref, high_ref, low_ref, g_ref, sc_ref, v_ref, acc_ref):
    step = pl.program_id(0)
    block, rows, length = x_ref.shape
    classes = vol_ref.shape[0]
    period = a_ref.shape[1]
    unit = ORIENTS and length // ORIENTS

    @pl.when(step == 0)
    def _():
        @pl.loop(0, classes)
        def _(k):
            spectrum = jnp.dot(vol_ref[k], fwd_ref[0:length, :], preferred_element_type=jnp.float32)
            v_ref[k] = spectrum.astype(jnp.bfloat16).astype(jnp.float32)
            acc_ref[k] = jnp.zeros(acc_ref.shape[1:], jnp.float32)

    for i in range(block):
        p = step * block + i
        k = cls_ref[p]
        start = pl.multiple_of(length - unit * ori_ref[p], unit)
        y = jnp.dot(x_ref[i], fwd_ref[pl.ds(start, length), :], preferred_element_type=jnp.float32)
        total = jnp.zeros((8, length), jnp.float32)
        for r in range(0, period, 8):
            a = a_ref[i, r : r + 8, :]
            for j in range(r, rows, period):
                for c in (0, length):
                    d = y[j : j + 8, c : c + length] - a * v_ref[k, j : j + 8, c : c + length]
                    total = total + d * d
                    acc_ref[k, j : j + 8, c : c + length] += a * d
        sc_ref[i, :] = jnp.sum(total, axis=0)

    @pl.when(step == pl.num_programs(0) - 1)
    def _():
        @pl.loop(0, classes)
        def _(k):
            s = acc_ref[k]
            s_high = s.astype(jnp.bfloat16)
            s_low = (s - s_high.astype(jnp.float32)).astype(jnp.bfloat16)
            g = jnp.dot(s_high, high_ref[...], preferred_element_type=jnp.float32)
            g += jnp.dot(s_low, high_ref[...], preferred_element_type=jnp.float32)
            g += jnp.dot(s_high, low_ref[...], preferred_element_type=jnp.float32)
            g_ref[k] = g.astype(jnp.bfloat16)


def main_call(x, a, vol, assignment, orientation, fwd, high, low):
    total, rows, length = x.shape
    classes = vol.shape[0]
    period = a.shape[1]
    whole = lambda *shape: pl.BlockSpec(shape, lambda i, *_: (0,) * len(shape))
    return pl.pallas_call(
        main_kernel,
        out_shape=(
            jax.ShapeDtypeStruct((classes, rows, length), jnp.bfloat16),
            jax.ShapeDtypeStruct((total, length), jnp.float32),
        ),
        grid_spec=pltpu.PrefetchScalarGridSpec(
            num_scalar_prefetch=2,
            grid=(total // BLOCK,),
            in_specs=[
                pl.BlockSpec((BLOCK, rows, length), lambda i, *_: (i, 0, 0)),
                pl.BlockSpec((BLOCK, period, length), lambda i, *_: (i, 0, 0)),
                whole(classes, rows, length),
                whole(2 * length, 2 * length),
                whole(2 * length, length),
                whole(2 * length, length),
            ],
            out_specs=[
                whole(classes, rows, length),
                pl.BlockSpec((BLOCK, length), lambda i, *_: (i, 0)),
            ],
            scratch_shapes=[
                pltpu.VMEM((classes, rows, 2 * length), jnp.float32),
                pltpu.VMEM((classes, rows, 2 * length), jnp.float32),
            ],
        ),
        compiler_params=pltpu.CompilerParams(vmem_limit_bytes=48 << 20),
        name="main",
    )(assignment, orientation, x, a, vol, fwd, high, low)


def local(particles, volumes, assignment, defocus, tilt_limits, orientation):
    total, rows, length = particles.shape
    fwd, high, low = tables(length)
    vol = lax.all_gather(volumes, "batch", axis=0, tiled=True)
    classes = vol.shape[0]
    period = length // 2
    first = lax.axis_index("cls") * rows
    radius = 1 + (first + jnp.arange(period, dtype=jnp.int32)) % period
    a = amplitudes(defocus, tilt_limits, radius, length)
    g, partial = main_call(particles, a, vol, assignment, orientation, fwd, high, low)
    scale = 1.0 / (rows * lax.axis_size("cls") * length * length)
    scores = lax.psum(jnp.sum(partial, axis=1) * scale, "cls")
    ids = jnp.arange(classes, dtype=jnp.int32)
    counts = jnp.sum((assignment[:, None] == ids[None, :]).astype(jnp.float32), axis=0)
    counts = lax.psum(counts, "batch")
    per = volumes.shape[0]
    mine = lax.dynamic_slice_in_dim(counts, lax.axis_index("batch") * per, per)
    grad = lax.psum_scatter(g, "batch", scatter_dimension=0, tiled=True).astype(jnp.float32)
    updated = volumes.astype(jnp.float32) + STEP * grad / (mine + 1.0)[:, None, None]
    return updated, scores


def solution(mesh):
    in_specs = (
        P("batch", "cls", None),
        P("batch", "cls", None),
        P("batch"),
        P("batch"),
        P("batch", None),
        P("batch"),
    )
    out_specs = (P("batch", "cls", None), P("batch"))
    return jax.shard_map(local, mesh=mesh, in_specs=in_specs, out_specs=out_specs, check_vma=False)
```

time: 374 us -> 154 us (0.41)
  the two profiles are of different devices: /device:TPU:1 before, /device:TPU:0 now
where the time goes in v1:
time: 154 us
  blocking collectives  65.5 us (43%)
  waiting for transfers between devices  36.4 us (24%)
  Pallas kernels  27.2 us (18%)
  between operations  14.8 us (10%)
  other arithmetic  7.24 us (5%)
  local copies, waits for them, and re-layouts  2.68 us (2%)
    psum x1, blocking collectives, local(): scores = lax.psum(jnp.sum(partial, axis=1) * scale, 'cls')  40.8 us
    all_gather x1, waiting for transfers between devices, local(): vol = lax.all_gather(volumes, 'batch', axis=0, tiled=True)  35.7 us
    pallas_call x1, Pallas kernels, main_call(): pl.pallas_call(main_kernel, out_shape=(jax.ShapeDtypeStruct((classes, row...  27.2 us
    psum x1, blocking collectives, local(): counts = lax.psum(counts, 'batch')  24.7 us
    select_n x1, other arithmetic, amplitudes(): return jnp.where(keep, ctf, 0.0)  4.03 us
  transfers between devices with their start and end apart: 2, of which 1 were waited for; matrix products, arithmetic and copies ran while one was open for 5% of the time, Pallas kernels for 0%

profile of v1, /device:TPU:0, one launch (start us, length us, event | category | flops | bytes accessed | tf_op | source)
XLA Modules:
  0.0 153.9 jit_solution(211672456448617555)
XLA Ops:
  7.2 0.0 copy-start.2
  7.2 0.0 copy-start.3
  7.2 0.0 copy-start.1
  7.2 0.0 copy-start.5
  7.2 0.0 copy-start.4
  7.2 0.0 all-gather.2.cloned.1.call-start
  7.3 0.7 all-gather.2.cloned.1.call-update
  8.0 0.0 reduce-scatter.2.cloned.1.call-start
  8.1 0.7 convert_multiply_fusion.1
  8.7 0.8 slice_bitcast_fusion.1
  9.5 0.1 broadcast_select_fusion
  9.6 0.3 fusion.1
  9.9 0.3 multiply_cosine_fusion
  10.2 4.0 %negate_select_fusion.a_ref = f32[128,64,128]{2,1,0:T(8,128)} fusion(f32[128,64]{1,0:T(8,128)S(1)} %get-tuple-element.11, f32[128,128]{1,0:T(8,128)S(1)} %get-tuple-element.9, f32[128,64]{1,0:T(8,128)S(1)} %get-tuple-element.10, f32[128,128]{1,0:T(8,128)S(1)} %get-tuple-element.8, s32[64]{0:T(128)S(1)} %fusion.2, s32[128,128]{1,0:T(8,128)S(1)} %broadcast_select_fusion, ...), kind=kLoop, calls=%fused_computation | loop fusion | flops 7340032 | bytes 4457216 | tf_op jit(solution)/shard_map/jit(_where)/select_n | solution.py:42
  14.2 35.7 %all-gather.2.cloned.1.call-done.vol_ref = bf16[16,320,128]{2,1,0:T(8,128)(2,1)} async-done(((bf16[1,320,128]{2,1,0:T(8,128)(2,1)}), bf16[16,320,128]{2,1,0:T(8,128)(2,1)}) %all-gather.2.cloned.1.call-update) | async-done | bytes 1310736 | tf_op jit(solution)/shard_map/all_gather | solution.py:127
  50.0 0.0 copy-done.2
  50.0 0.0 copy-done.3
  50.0 0.0 copy-done.1
  50.0 0.0 copy-done.5
  50.0 0.0 copy-done.4
  50.0 0.0 copy-start
  50.0 1.3 copy-done
  51.3 0.0 copy-start.6
  51.3 27.2 %main.1 = (bf16[16,320,128]{2,1,0:T(8,128)(2,1)}, f32[128,128]{1,0:T(8,128)S(1)}) custom-call(s32[128]{0:T(128)S(1)} %copy-done.5, s32[128]{0:T(128)S(1)} %copy-done.4, bf16[128,320,128]{2,1,0:T(8,128)(2,1)} %x_ref.1, f32[128,64,128]{2,1,0:T(8,128)} %negate_select_fusion.a_ref, bf16[16,320,128]{2,1,0:T(8,128)(2,1)S(1)} %copy-done, ...), custom_call_target="tpu_custom_call" | custom-call | tf_op jit(solution)/shard_map/main/pallas_call | solution.py:93
  78.5 0.0 reduce-scatter.2.cloned.1.call-update
  78.5 0.1 convert_reduce_fusion
  78.6 24.7 %psum.14 = f32[16]{0:T(128)S(1)} all-reduce(f32[16]{0:T(128)S(1)} %convert_reduce_fusion), channel_id=1, replica_groups=mesh['cls'=16,'batch'=16] {'batch'}, use_global_device_ids=true, to_apply=%region_2.3 | all-reduce | flops 16 | bytes 128 | tf_op jit(solution)/shard_map/psum | solution.py:138
  103.3 0.6 dynamic_slice.3
  104.5 0.1 reduce_sum.19
  104.7 40.8 %psum.15 = f32[128]{0:T(128)} all-reduce(f32[128]{0:T(128)S(1)} %broadcast_multiply_fusion), channel_id=1, replica_groups=mesh['cls'=16,'batch'=16] {'cls'}, use_global_device_ids=true, to_apply=%region_4.5 | all-reduce | flops 128 | bytes 1024 | tf_op jit(solution)/shard_map/psum | solution.py:135
  145.5 0.0 reduce-scatter.2.cloned.1.call-done
  145.5 0.0 copy-done.6
  145.5 1.6 %divide_add_fusion = f32[1,320,128]{2,1,0:T(8,128)} fusion(bf16[1,320,128]{2,1,0:T(8,128)(2,1)} %reduce-scatter.2.cloned.1.call-done, bf16[1,320,128]{2,1,0:T(8,128)(2,1)S(1)} %copy-done.6, f32[]{:T(128)} %bitcast.2), kind=kLoop, calls=%fused_computation.2 | loop fusion | flops 204800 | bytes 327684 | tf_op jit(solution)/shard_map/add | solution.py:142
  (5 shorter events, 0.0 us)
Async XLA Ops:
  7.2 42.8 %copy-start.2 = (bf16[256,128]{1,0:T(8,128)(2,1)S(1)}, bf16[256,128]{1,0:T(8,128)(2,1)}, u32[]{:S(2)}) copy-start(bf16[256,128]{1,0:T(8,128)(2,1)} %constant.66.low_ref) | copy-start | bytes 196612
  7.2 42.8 %copy-start.3 = (bf16[256,128]{1,0:T(8,128)(2,1)S(1)}, bf16[256,128]{1,0:T(8,128)(2,1)}, u32[]{:S(2)}) copy-start(bf16[256,128]{1,0:T(8,128)(2,1)} %constant.63.high_ref) | copy-start | bytes 196612
  7.2 42.8 %copy-start.1 = (bf16[256,256]{1,0:T(8,128)(2,1)S(1)}, bf16[256,256]{1,0:T(8,128)(2,1)}, u32[]{:S(2)}) copy-start(bf16[256,256]{1,0:T(8,128)(2,1)} %constant.62.fwd_ref) | copy-start | bytes 393220
  7.2 42.8 %copy-start.5 = (s32[128]{0:T(128)S(1)}, s32[128]{0:T(128)}, u32[]{:S(2)}) copy-start(s32[128]{0:T(128)} %cls_ref.1) | copy-start | bytes 1540
  7.2 42.8 %copy-start.4 = (s32[128]{0:T(128)S(1)}, s32[128]{0:T(128)}, u32[]{:S(2)}) copy-start(s32[128]{0:T(128)} %ori_ref.1) | copy-start | bytes 1540
  7.2 42.8 %all-gather.2.cloned.1.call-start = ((), (), s32[]{:S(2)}) async-start(), calls=%async_computation.1 | async-start | bytes 1392640 | tf_op jit(solution)/shard_map/all_gather | solution.py:127
  8.0 137.5 %reduce-scatter.2.cloned.1.call-start = ((), (), s32[]{:S(2)}) async-start(), calls=%async_computation.2 | async-start | bytes 1392640 | tf_op jit(solution)/shard_map/reduce_scatter | solution.py:141
  50.0 1.3 copy-start
  51.3 94.2 %copy-start.6 = (bf16[1,320,128]{2,1,0:T(8,128)(2,1)S(1)}, bf16[1,320,128]{2,1,0:T(8,128)(2,1)}, u32[]{:S(2)}) copy-start(bf16[1,320,128]{2,1,0:T(8,128)(2,1)} %param.9) | copy-start | bytes 245764
Sparse Core Ops, SparseCore 0:
  9.9 40.0 all-gather.1
  78.6 57.3 reduce-scatter.1

commit v2 on v1

--- a/solution.py
+++ b/solution.py
@@ -1,3 +1,4 @@
+import functools
 import math
 
 import jax
@@ -27,25 +28,354 @@
     return turned, high, low
 
 
-def amplitudes(defocus, tilt_limits, radius, length):
-    freq = jnp.arange(length, dtype=jnp.int32)
+MESH = pl.DeviceIdType.MESH
+
+
+def sine_terms(count):
+    u = np.cos(np.pi * (np.arange(4000) + 0.5) / 4000) * 0.5
+    u = u[np.abs(u) > 1e-6]
+    basis = np.stack([u ** (2 * i + 1) for i in range(count)], axis=1)
+    return [float(c) for c in np.linalg.lstsq(basis, -np.sin(2 * np.pi * u), rcond=None)[0]]
+
+
+def gather_kernel(
+    defocus_ref, tilt_ref, vol_ref, counts_ref, fwd_ref, v_out, a_out, counts_out,
+    buf, v_buf, a_buf, own_sem, v_sem, a_sem, ring_send, ring_recv, pair_send, pair_recv,
+):
+    devices, _, length = buf.shape
+    rows = vol_ref.shape[1]
+    total, period, _ = a_buf.shape
+    depth = devices // 2
+    far = depth // 2
+    me = lax.axis_index("batch")
+    z, core = me // 2, me % 2
+    other = 1 - core
+    right = ((z + 1) % depth) * 2 + core
+    left = ((z + depth - 1) % depth) * 2 + core
+    partner = z * 2 + other
+    spans = ((0, rows // 2), (rows // 2, buf.shape[1] - rows // 2))
+
+    own = (
+        pltpu.make_async_copy(vol_ref.at[0], buf.at[me, pl.ds(0, rows)], own_sem.at[0]),
+        pltpu.make_async_copy(counts_ref, buf.at[me, pl.ds(rows, counts_ref.shape[0])], own_sem.at[1]),
+    )
+    for copy in own:
+        copy.start()
+    barrier = pltpu.get_barrier_semaphore()
+    for peer in (left, right, partner):
+        pl.semaphore_signal(barrier, inc=1, device_id={"batch": peer}, device_id_type=MESH)
+    pl.semaphore_wait(barrier, 3)
+    for copy in own:
+        copy.wait()
+
+    def halves(way, s):
+        return (0, 1) if s < far else ((0,) if way == 0 else (1,))
+
+    def owner(way, s):
+        return (z + depth - s) % depth if way == 0 else (z + s) % depth
+
+    def unit(way, s, h):
+        return way * 2 * far + (s - 1) * 2 + h
+
+    def ring(way, s, h):
+        at = buf.at[owner(way, s - 1) * 2 + core, pl.ds(*spans[h])]
+        i = unit(way, s, h)
+        return pltpu.make_async_remote_copy(
+            src_ref=at, dst_ref=at, send_sem=ring_send.at[i], recv_sem=ring_recv.at[i],
+            device_id={"batch": right if way == 0 else left}, device_id_type=MESH,
+        )
+
+    def arrival(way, s, h):
+        at = buf.at[owner(way, s) * 2 + core, pl.ds(*spans[h])]
+        i = unit(way, s, h)
+        return pltpu.make_async_remote_copy(
+            src_ref=at, dst_ref=at, send_sem=ring_send.at[i], recv_sem=ring_recv.at[i],
+            device_id={"batch": right if way == 0 else left}, device_id_type=MESH,
+        )
+
+    def pair(zz, i, h, which):
+        at = buf.at[zz * 2 + which, pl.ds(*spans[h])]
+        return pltpu.make_async_remote_copy(
+            src_ref=at, dst_ref=at, send_sem=pair_send.at[i], recv_sem=pair_recv.at[i],
+            device_id={"batch": partner}, device_id_type=MESH,
+        )
+
+    sent = []
+    own_unit = 4 * far
+    for h in (0, 1):
+        for way in (0, 1):
+            if h in halves(way, 1):
+                sent.append(ring(way, 1, h))
+                sent[-1].start()
+    for h in (0, 1):
+        sent.append(pair(z, own_unit + h, h, core))
+        sent[-1].start()
+
+    freq = lax.broadcasted_iota(jnp.int32, (8, length), 1)
     signed = jnp.where(freq < length // 2, freq, freq - length)
+    reach = (8 * jnp.abs(signed)).astype(jnp.float32)
+    squares = (signed * signed).astype(jnp.float32)
+    row = lax.broadcasted_iota(jnp.int32, (8, length), 0)
+    radii = [(row + (1 + r)).astype(jnp.float32) for r in range(0, period, 8)]
     half = length // 2
-    along_s = math.pi * defocus[:, None] * ((signed * signed).astype(jnp.float32) / float(half * half))[None, :] + PHASE
-    along_r = math.pi * defocus[:, None] * ((radius * radius).astype(jnp.float32) / float(half * half))[None, :]
-    ctf = -(
-        jnp.sin(along_s)[:, None, :] * jnp.cos(along_r)[:, :, None]
-        + jnp.cos(along_s)[:, None, :] * jnp.sin(along_r)[:, :, None]
+    grid = [(squares + r * r) * (0.5 / (half * half)) for r in radii]
+    terms = sine_terms(8)
+    share = total // (far + 1)
+    parts = [(q * share, share if q < far else total - far * share) for q in range(far + 1)]
+    a_copies = []
+
+    def filters(q):
+        first, number = parts[q]
+
+        def body(i, carry):
+            p = first + i
+            d = defocus_ref[p]
+            limit = jnp.where(freq < length // 2, tilt_ref[2 * p], tilt_ref[2 * p + 1]).astype(jnp.float32)
+            for n in range(period // 8):
+                turns = d * grid[n] + PHASE / (2.0 * math.pi)
+                u = turns - jnp.floor(turns + 0.5)
+                w = u * u
+                s = jnp.full_like(w, terms[-1])
+                for c in terms[-2::-1]:
+                    s = s * w + c
+                a_buf[p, 8 * n : 8 * n + 8, :] = jnp.where(reach <= limit * radii[n], s * u, 0.0)
+            return carry
+
+        lax.fori_loop(0, number, body, 0)
+        copy = pltpu.make_async_copy(a_buf.at[pl.ds(first, number)], a_out.at[pl.ds(first, number)], a_sem.at[q])
+        copy.start()
+        a_copies.append(copy)
+
+    v_copies = []
+
+    def transform(slot, i):
+        spectrum = jnp.dot(buf[slot, 0:rows, :], fwd_ref[0:length, :], preferred_element_type=jnp.float32)
+        v_buf[slot] = spectrum.astype(jnp.bfloat16)
+        copy = pltpu.make_async_copy(v_buf.at[slot], v_out.at[slot], v_sem.at[i])
+        copy.start()
+        v_copies.append(copy)
+
+    def from_pair(s):
+        if s == 0:
+            for h in (0, 1):
+                pair(z, own_unit + h, h, other).wait_recv()
+            transform(partner, len(v_copies))
+            return
+        for way in (0, 1):
+            for h in halves(way, s):
+                pair(owner(way, s), unit(way, s, h), h, other).wait_recv()
+        for way in (0, 1) if s < far else (0,):
+            transform(owner(way, s) * 2 + other, len(v_copies))
+
+    filters(0)
+    transform(me, 0)
+    for s in range(1, far + 1):
+        for h in (0, 1):
+            for way in (0, 1):
+                if h not in halves(way, s):
+                    continue
+                arrival(way, s, h).wait_recv()
+                if s < far and h in halves(way, s + 1):
+                    sent.append(ring(way, s + 1, h))
+                    sent[-1].start()
+                sent.append(pair(owner(way, s), unit(way, s, h), h, core))
+                sent[-1].start()
+        filters(s)
+        for way in (0, 1) if s < far else (0,):
+            transform(owner(way, s) * 2 + core, len(v_copies))
+        from_pair(s - 1)
+    from_pair(far)
+    tally = jnp.zeros((8, length), jnp.float32)
+    for b in range(devices):
+        tally += buf[b, rows : rows + 8, :].astype(jnp.float32)
+    counts_out[...] = tally
+    for copy in sent:
+        copy.wait_send()
+    for copy in v_copies + a_copies:
+        copy.wait()
+
+
+def gather_call(volumes, counts, defocus, tilts, fwd, devices):
+    _, rows, length = volumes.shape
+    total = defocus.shape[0]
+    period = length // 2
+    anywhere = pl.BlockSpec(memory_space=pl.ANY)
+    scalars = pl.BlockSpec(memory_space=pltpu.SMEM)
+    inside = pl.BlockSpec(memory_space=pltpu.VMEM)
+    units = 2 * devices
+    return pl.pallas_call(
+        gather_kernel,
+        out_shape=(
+            jax.ShapeDtypeStruct((devices, rows, 2 * length), jnp.bfloat16),
+            jax.ShapeDtypeStruct((total, period, length), jnp.float32),
+            jax.ShapeDtypeStruct((8, length), jnp.float32),
+        ),
+        in_specs=[scalars, scalars, anywhere, anywhere, inside],
+        out_specs=(anywhere, anywhere, inside),
+        scratch_shapes=[
+            pltpu.VMEM((devices, rows + counts.shape[0], length), jnp.bfloat16),
+            pltpu.VMEM((devices, rows, 2 * length), jnp.bfloat16),
+            pltpu.VMEM((total, period, length), jnp.float32),
+            pltpu.SemaphoreType.DMA((2,)),
+            pltpu.SemaphoreType.DMA((devices,)),
+            pltpu.SemaphoreType.DMA((devices // 4 + 1,)),
+            pltpu.SemaphoreType.DMA((units,)),
+            pltpu.SemaphoreType.DMA((units,)),
+            pltpu.SemaphoreType.DMA((units,)),
+            pltpu.SemaphoreType.DMA((units,)),
+        ],
+        compiler_params=pltpu.CompilerParams(collective_id=0, has_side_effects=True, vmem_limit_bytes=40 << 20),
+        name="gather",
+    )(defocus, tilts, volumes, counts, fwd)
+
+
+def reduce_kernel(
+    side, scale, g_ref, vol_ref, sc_ref, counts_ref, new_ref, scores_ref,
+    from_pair, came, going, across, down,
+    pair_send, pair_recv, ring_send, ring_recv, across_send, across_recv, down_send, down_recv,
+):
+    devices, rows, length = g_ref.shape
+    depth = devices // 2
+    far = depth // 2
+    me = lax.axis_index("batch")
+    z, core = me // 2, me % 2
+    other = 1 - core
+    right = ((z + 1) % depth) * 2 + core
+    left = ((z + depth - 1) % depth) * 2 + core
+    partner = z * 2 + other
+    c = lax.axis_index("cls")
+    y, x = c // side, c % side
+    in_row = [y * side + (x + d) % side for d in range(1, side)]
+    in_column = [((y + d) % side) * side + x for d in range(1, side)]
+
+    barrier = pltpu.get_barrier_semaphore()
+    for peer in (left, right, partner):
+        pl.semaphore_signal(barrier, inc=1, device_id={"batch": peer}, device_id_type=MESH)
+    for peer in in_row + in_column:
+        pl.semaphore_signal(barrier, inc=1, device_id={"cls": peer}, device_id_type=MESH)
+    pl.semaphore_wait(barrier, 3 + 2 * (side - 1))
+
+    order = [far]
+    for d in range(far - 1, 0, -1):
+        order += [d, depth - d]
+    order.append(0)
+    pairs = {}
+    for i, d in enumerate(order):
+        j = (z + d) % depth
+        pairs[d] = pltpu.make_async_remote_copy(
+            src_ref=g_ref.at[2 * j + other], dst_ref=from_pair.at[j],
+            send_sem=pair_send.at[i], recv_sem=pair_recv.at[i],
+            device_id={"batch": partner}, device_id_type=MESH,
+        )
+        pairs[d].start()
+
+    def spread(ref, send, recv, peers, axis):
+        copies = []
+        for d, peer in enumerate(peers, 1):
+            copies.append(pltpu.make_async_remote_copy(
+                src_ref=ref.at[0], dst_ref=ref.at[d], send_sem=send.at[d - 1], recv_sem=recv.at[d - 1],
+                device_id={axis: peer}, device_id_type=MESH,
+            ))
+            copies[-1].start()
+        return copies
+
+    across[0] = lax.dot_general(
+        jnp.full((8, length), scale, jnp.float32), sc_ref[...], (((1,), (1,)), ((), ())),
+        precision=lax.Precision.HIGHEST, preferred_element_type=jnp.float32,
     )
-    limit = jnp.where(signed[None, :] >= 0, tilt_limits[:, 0][:, None], tilt_limits[:, 1][:, None])
-    keep = 8 * jnp.abs(signed)[None, None, :] <= limit[:, None, :] * radius[None, :, None]
-    return jnp.where(keep, ctf, 0.0)
-
-
-def main_kernel(cls_ref, ori_ref, x_ref, a_ref, vol_ref, fwd_ref, high_ref, low_ref, g_ref, sc_ref, v_ref, acc_ref):
+    row_copies = spread(across, across_send, across_recv, in_row, "cls")
+
+    spans = (pl.ds(0, rows // 2), pl.ds(rows // 2, rows // 2))
+
+    def mine(j, h):
+        return g_ref[2 * j + core, spans[h], :].astype(jnp.float32) + from_pair[j, spans[h], :].astype(jnp.float32)
+
+    def began(way, s, h):
+        return s > 1 or h == way
+
+    def ring(way, s, h):
+        i = way * 2 * far + (s - 1) * 2 + h
+        return pltpu.make_async_remote_copy(
+            src_ref=going.at[way, s - 1, spans[h]], dst_ref=came.at[way, s - 1, spans[h]],
+            send_sem=ring_send.at[i], recv_sem=ring_recv.at[i],
+            device_id={"batch": right if way == 0 else left}, device_id_type=MESH,
+        )
+
+    sent = []
+    column_copies = None
+    for s in range(1, far + 1):
+        d = far + 1 - s
+        for e in {d, (depth - d) % depth}:
+            pairs[e].wait_recv()
+        for h in (0, 1):
+            for way in (0, 1):
+                if not began(way, s, h):
+                    continue
+                j = (z + d) % depth if way == 0 else (z + depth - d) % depth
+                value = mine(j, h)
+                if s > 1 and began(way, s - 1, h):
+                    ring(way, s - 1, h).wait_recv()
+                    value += came[way, s - 2, spans[h], :].astype(jnp.float32)
+                going[way, s - 1, spans[h], :] = value.astype(jnp.bfloat16)
+                sent.append(ring(way, s, h))
+                sent[-1].start()
+        if s == 2:
+            for copy in row_copies:
+                copy.wait_recv()
+            down[0] = sum(across[d] for d in range(1, side)) + across[0]
+            column_copies = spread(down, down_send, down_recv, in_column, "cls")
+
+    lane = lax.broadcasted_iota(jnp.int32, (1, length), 1)
+    count = jnp.sum(jnp.where(lane == me, counts_ref[0:1, :], 0.0), axis=1, keepdims=True)
+    factor = STEP / (count + 1.0)
+    pairs[0].wait_recv()
+    for h in (0, 1):
+        value = mine(z, h)
+        for way in (0, 1):
+            ring(way, far, h).wait_recv()
+            value += came[way, far - 1, spans[h], :].astype(jnp.float32)
+        new_ref[0, spans[h], :] = vol_ref[0, spans[h], :].astype(jnp.float32) + value * factor
+    for copy in column_copies:
+        copy.wait_recv()
+    scores_ref[...] = sum(down[d] for d in range(1, side)) + down[0]
+    for copy in sent + row_copies + column_copies + list(pairs.values()):
+        copy.wait_send()
+
+
+def reduce_call(g, volumes, partial, counts, scale, lanes):
+    devices, rows, length = g.shape
+    depth = devices // 2
+    far = depth // 2
+    side = math.isqrt(lanes)
+    inside = pl.BlockSpec(memory_space=pltpu.VMEM)
+    sems = lambda n: pltpu.SemaphoreType.DMA((n,))
+    peers = max(side - 1, 1)
+    return pl.pallas_call(
+        functools.partial(reduce_kernel, side, scale),
+        out_shape=(
+            jax.ShapeDtypeStruct((1, rows, length), jnp.float32),
+            jax.ShapeDtypeStruct((8, partial.shape[0]), jnp.float32),
+        ),
+        in_specs=[inside] * 4,
+        out_specs=(inside, inside),
+        scratch_shapes=[
+            pltpu.VMEM((depth, rows, length), jnp.bfloat16),
+            pltpu.VMEM((2, far, rows, length), jnp.bfloat16),
+            pltpu.VMEM((2, far, rows, length), jnp.bfloat16),
+            pltpu.VMEM((side, 8, partial.shape[0]), jnp.float32),
+            pltpu.VMEM((side, 8, partial.shape[0]), jnp.float32),
+            sems(depth), sems(depth), sems(4 * far), sems(4 * far),
+            sems(peers), sems(peers), sems(peers), sems(peers),
+        ],
+        compiler_params=pltpu.CompilerParams(collective_id=1, has_side_effects=True, vmem_limit_bytes=24 << 20),
+        name="reduce",
+    )(g, volumes, partial, counts)
+
+
+def main_kernel(cls_ref, ori_ref, x_ref, a_ref, spec_ref, fwd_ref, high_ref, low_ref, g_ref, sc_ref, v_ref, acc_ref):
     step = pl.program_id(0)
     block, rows, length = x_ref.shape
-    classes = vol_ref.shape[0]
+    classes = spec_ref.shape[0]
     period = a_ref.shape[1]
     unit = ORIENTS and length // ORIENTS
 
@@ -53,8 +383,7 @@
     def _():
         @pl.loop(0, classes)
         def _(k):
-            spectrum = jnp.dot(vol_ref[k], fwd_ref[0:length, :], preferred_element_type=jnp.float32)
-            v_ref[k] = spectrum.astype(jnp.bfloat16).astype(jnp.float32)
+            v_ref[k] = spec_ref[k].astype(jnp.float32)
             acc_ref[k] = jnp.zeros(acc_ref.shape[1:], jnp.float32)
 
     for i in range(block):
@@ -85,9 +414,9 @@
             g_ref[k] = g.astype(jnp.bfloat16)
 
 
-def main_call(x, a, vol, assignment, orientation, fwd, high, low):
+def main_call(x, a, spectra, assignment, orientation, fwd, high, low):
     total, rows, length = x.shape
-    classes = vol.shape[0]
+    classes = spectra.shape[0]
     period = a.shape[1]
     whole = lambda *shape: pl.BlockSpec(shape, lambda i, *_: (0,) * len(shape))
     return pl.pallas_call(
@@ -102,7 +431,7 @@
             in_specs=[
                 pl.BlockSpec((BLOCK, rows, length), lambda i, *_: (i, 0, 0)),
                 pl.BlockSpec((BLOCK, period, length), lambda i, *_: (i, 0, 0)),
-                whole(classes, rows, length),
+                whole(classes, rows, 2 * length),
                 whole(2 * length, 2 * length),
                 whole(2 * length, length),
                 whole(2 * length, length),
@@ -118,29 +447,23 @@
         ),
         compiler_params=pltpu.CompilerParams(vmem_limit_bytes=48 << 20),
         name="main",
-    )(assignment, orientation, x, a, vol, fwd, high, low)
+    )(assignment, orientation, x, a, spectra, fwd, high, low)
 
 
 def local(particles, volumes, assignment, defocus, tilt_limits, orientation):
     total, rows, length = particles.shape
+    devices = lax.axis_size("batch")
+    lanes = lax.axis_size("cls")
+    assert volumes.shape[0] == 1 and rows % (length // 2) == 0
     fwd, high, low = tables(length)
-    vol = lax.all_gather(volumes, "batch", axis=0, tiled=True)
-    classes = vol.shape[0]
-    period = length // 2
-    first = lax.axis_index("cls") * rows
-    radius = 1 + (first + jnp.arange(period, dtype=jnp.int32)) % period
-    a = amplitudes(defocus, tilt_limits, radius, length)
-    g, partial = main_call(particles, a, vol, assignment, orientation, fwd, high, low)
-    scale = 1.0 / (rows * lax.axis_size("cls") * length * length)
-    scores = lax.psum(jnp.sum(partial, axis=1) * scale, "cls")
-    ids = jnp.arange(classes, dtype=jnp.int32)
+    ids = jnp.arange(length, dtype=jnp.int32)
     counts = jnp.sum((assignment[:, None] == ids[None, :]).astype(jnp.float32), axis=0)
-    counts = lax.psum(counts, "batch")
-    per = volumes.shape[0]
-    mine = lax.dynamic_slice_in_dim(counts, lax.axis_index("batch") * per, per)
-    grad = lax.psum_scatter(g, "batch", scatter_dimension=0, tiled=True).astype(jnp.float32)
-    updated = volumes.astype(jnp.float32) + STEP * grad / (mine + 1.0)[:, None, None]
-    return updated, scores
+    counts = jnp.broadcast_to(counts.astype(jnp.bfloat16)[None, :], (16, length))
+    spectra, a, tally = gather_call(volumes, counts, defocus, tilt_limits.reshape(-1), fwd, devices)
+    g, partial = main_call(particles, a, spectra, assignment, orientation, fwd, high, low)
+    scale = 1.0 / (rows * lanes * length * length)
+    updated, scores = reduce_call(g, volumes, partial, tally, scale, lanes)
+    return updated, scores[0]
 
 
 def solution(mesh):

time: 154 us -> 80.1 us (0.52)
  the two profiles are of different devices: /device:TPU:0 before, /device:TPU:1 now
where the time goes in v2:
time: 80.1 us; the launch traced here: 79.5 us
  Pallas kernels  67.7 us (85%)
  local copies, waits for them, and re-layouts  10.4 us (13%)
    pallas_call x1, Pallas kernels, gather_call(): pl.pallas_call(gather_kernel, out_shape=(jax.ShapeDtypeStruct((devices, r...  24.3 us
    pallas_call x1, Pallas kernels, main_call(): pl.pallas_call(main_kernel, out_shape=(jax.ShapeDtypeStruct((classes, row...  23.7 us
    pallas_call x1, Pallas kernels, reduce_call(): pl.pallas_call(functools.partial(reduce_kernel, side, scale), out_shape=(...  19.6 us
    unnamed x22, local copies, waits for them, and re-layouts  9.73 us

profile of v2, /device:TPU:1, one launch (start us, length us, event | category | flops | bytes accessed | tf_op | source)
XLA Modules:
  0.0 79.5 jit_solution(5617357701420929171)
XLA Ops:
  0.6 0.8 convert_reduce_fusion
  1.4 0.8 copy.11
  2.2 0.1 reshape.11.tilt_ref
  2.3 0.0 copy-start.1
  2.3 0.9 %copy-done.1 = bf16[256,256]{1,0:T(8,128)(2,1)S(1)} copy-done((bf16[256,256]{1,0:T(8,128)(2,1)S(1)}, bf16[256,256]{1,0:T(8,128)(2,1)}, u32[]{:S(2)}) %copy-start.1) | copy-done | bytes 131096
  3.2 0.0 copy-start.3
  3.2 0.9 %copy-done.3 = bf16[1,320,128]{2,1,0:T(8,128)(2,1)S(1)} copy-done((bf16[1,320,128]{2,1,0:T(8,128)(2,1)S(1)}, bf16[1,320,128]{2,1,0:T(8,128)(2,1)}, u32[]{:S(2)}) %copy-start.3) | copy-done | bytes 81944
  4.1 0.0 copy-start.7
  4.1 0.7 copy-done.7
  4.8 24.3 %gather.1 = (bf16[16,320,256]{2,1,0:T(8,128)(2,1)S(1)}, f32[128,64,128]{2,1,0:T(8,128)S(1)}, f32[8,128]{1,0:T(8,128)S(1)}) custom-call(f32[128]{0:T(128)S(1)} %copy-done.7, s32[256]{0:T(256)S(1)} %reshape.11.tilt_ref, bf16[1,320,128]{2,1,0:T(8,128)(2,1)S(1)} %copy-done.3, bf16[16,128]{1,0:T(8,128)(2,1)S(1)} %broadcast_in_dim.2.counts_ref, ...), custom_call_target="tpu_custom_call" | custom-call | tf_op jit(solution)/shard_map/gather/pallas_call | solution.py:206
  29.1 0.0 copy-start
  29.1 1.9 %copy-done = f32[128,64,128]{2,1,0:T(8,128)} copy-done((f32[128,64,128]{2,1,0:T(8,128)}, f32[128,64,128]{2,1,0:T(8,128)S(1)}, u32[]{:S(2)}) %copy-start) | copy-done | bytes 4194328
  31.0 0.0 copy-start.2
  31.0 0.9 %copy-done.2 = bf16[256,256]{1,0:T(8,128)(2,1)S(1)} copy-done((bf16[256,256]{1,0:T(8,128)(2,1)S(1)}, bf16[256,256]{1,0:T(8,128)(2,1)}, u32[]{:S(2)}) %copy-start.2) | copy-done | bytes 131096
  31.9 0.0 copy-start.5
  31.9 0.8 %copy-done.5 = bf16[256,128]{1,0:T(8,128)(2,1)S(1)} copy-done((bf16[256,128]{1,0:T(8,128)(2,1)S(1)}, bf16[256,128]{1,0:T(8,128)(2,1)}, u32[]{:S(2)}) %copy-start.5) | copy-done | bytes 65560
  32.8 0.0 copy-start.6
  32.8 0.8 %copy-done.6 = bf16[256,128]{1,0:T(8,128)(2,1)S(1)} copy-done((bf16[256,128]{1,0:T(8,128)(2,1)S(1)}, bf16[256,128]{1,0:T(8,128)(2,1)}, u32[]{:S(2)}) %copy-start.6) | copy-done | bytes 65560
  33.6 0.0 copy-start.8
  33.6 0.7 copy-done.8
  34.3 0.0 copy-start.9
  34.3 0.7 copy-done.9
  34.9 0.0 copy-start.4
  34.9 23.7 %main.1 = (bf16[16,320,128]{2,1,0:T(8,128)(2,1)S(1)}, f32[128,128]{1,0:T(8,128)S(1)}) custom-call(s32[128]{0:T(128)S(1)} %copy-done.8, s32[128]{0:T(128)S(1)} %copy-done.9, bf16[128,320,128]{2,1,0:T(8,128)(2,1)} %x_ref.1, f32[128,64,128]{2,1,0:T(8,128)} %copy-done, bf16[16,320,256]{2,1,0:T(8,128)(2,1)S(1)} %get-tuple-element.10.spec_ref, ...), custom_call_target="tpu_custom_call" | custom-call | tf_op jit(solution)/shard_map/main/pallas_call | solution.py:422
  58.7 0.0 copy-done.4
  58.7 19.6 %reduce.1 = (f32[1,320,128]{2,1,0:T(8,128)S(1)}, f32[8,128]{1,0:T(8,128)S(1)}) custom-call(bf16[16,320,128]{2,1,0:T(8,128)(2,1)S(1)} %get-tuple-element.11.g_ref, bf16[1,320,128]{2,1,0:T(8,128)(2,1)S(1)} %copy-done.4, f32[128,128]{1,0:T(8,128)S(1)} %get-tuple-element.12.sc_ref, f32[8,128]{1,0:T(8,128)S(1)} %get-tuple-element.13.counts_ref), custom_call_target="tpu_custom_call" | custom-call | tf_op jit(solution)/shard_map/reduce/pallas_call | solution.py:353
  78.3 0.5 slice_bitcast_fusion
  78.8 0.7 copy.13
  (1 shorter events, 0.0 us)
Async XLA Ops:
  2.3 0.9 %copy-start.1 = (bf16[256,256]{1,0:T(8,128)(2,1)S(1)}, bf16[256,256]{1,0:T(8,128)(2,1)}, u32[]{:S(2)}) copy-start(bf16[256,256]{1,0:T(8,128)(2,1)} %constant.9.fwd_ref) | copy-start | bytes 393220
  3.2 0.9 %copy-start.3 = (bf16[1,320,128]{2,1,0:T(8,128)(2,1)S(1)}, bf16[1,320,128]{2,1,0:T(8,128)(2,1)}, u32[]{:S(2)}) copy-start(bf16[1,320,128]{2,1,0:T(8,128)(2,1)} %vol_ref.3) | copy-start | bytes 245764
  4.1 0.7 copy-start.7
  29.1 1.9 %copy-start = (f32[128,64,128]{2,1,0:T(8,128)}, f32[128,64,128]{2,1,0:T(8,128)S(1)}, u32[]{:S(2)}) copy-start(f32[128,64,128]{2,1,0:T(8,128)S(1)} %get-tuple-element.9.a_ref) | copy-start | bytes 12582916
  31.0 0.9 %copy-start.2 = (bf16[256,256]{1,0:T(8,128)(2,1)S(1)}, bf16[256,256]{1,0:T(8,128)(2,1)}, u32[]{:S(2)}) copy-start(bf16[256,256]{1,0:T(8,128)(2,1)} %constant.9.fwd_ref) | copy-start | bytes 393220
  31.9 0.8 %copy-start.5 = (bf16[256,128]{1,0:T(8,128)(2,1)S(1)}, bf16[256,128]{1,0:T(8,128)(2,1)}, u32[]{:S(2)}) copy-start(bf16[256,128]{1,0:T(8,128)(2,1)} %constant.13.low_ref) | copy-start | bytes 196612
  32.8 0.8 %copy-start.6 = (bf16[256,128]{1,0:T(8,128)(2,1)S(1)}, bf16[256,128]{1,0:T(8,128)(2,1)}, u32[]{:S(2)}) copy-start(bf16[256,128]{1,0:T(8,128)(2,1)} %constant.10.high_ref) | copy-start | bytes 196612
  33.6 0.7 copy-start.8
  34.3 0.7 copy-start.9
  34.9 23.7 %copy-start.4 = (bf16[1,320,128]{2,1,0:T(8,128)(2,1)S(1)}, bf16[1,320,128]{2,1,0:T(8,128)(2,1)}, u32[]{:S(2)}) copy-start(bf16[1,320,128]{2,1,0:T(8,128)(2,1)} %vol_ref.3) | copy-start | bytes 245764

commit v3 on v2

v3 whole, which is shorter than its diff:
```python
import functools
import math

import jax
import jax.numpy as jnp
import numpy as np
from jax import lax
from jax.experimental import pallas as pl
from jax.experimental.pallas import tpu as pltpu
from jax.sharding import PartitionSpec as P

ORIENTS = 8
STEP = 0.5
PHASE = 0.1
BLOCK = 8


def tables(length):
    index = np.arange(length)
    angle = 2.0 * np.pi * ((index[:, None] * index[None, :]) % length) / length
    cosine, sine = np.cos(angle), np.sin(angle)
    forward = np.concatenate([cosine, -sine], axis=1).astype(np.float32)
    back = (np.concatenate([cosine, -sine], axis=0) / length).astype(np.float32)
    turned = jnp.asarray(np.concatenate([forward, forward], axis=0)).astype(jnp.bfloat16)
    back = jnp.asarray(back)
    high = back.astype(jnp.bfloat16)
    low = (back - high.astype(jnp.float32)).astype(jnp.bfloat16)
    return jnp.concatenate([turned, high, low], axis=1)


MESH = pl.DeviceIdType.MESH


def sine_terms(count):
    u = np.cos(np.pi * (np.arange(4000) + 0.5) / 4000) * 0.5
    u = u[np.abs(u) > 1e-6]
    basis = np.stack([u ** (2 * i + 1) for i in range(count)], axis=1)
    return [float(c) for c in np.linalg.lstsq(basis, -np.sin(2 * np.pi * u), rcond=None)[0]]


def gather_kernel(
    defocus_in, tilt_in, class_in, vol_ref, table_ref, v_out, a_out, counts_out,
    buf, v_buf, a_buf, tally_buf, fwd_ref, tilt_ref, defocus_ref, class_ref,
    own_sem, v_sem, a_sem, ring_send, ring_recv, pair_send, pair_recv,
):
    devices, _, length = buf.shape
    rows = vol_ref.shape[1]
    total, period, _ = a_buf.shape
    depth = devices // 2
    far = depth // 2
    me = lax.axis_index("batch")
    z, core = me // 2, me % 2
    other = 1 - core
    partner = z * 2 + other

    def at_distance(way, d):
        return (z + d) % depth if way == 0 else (z + depth - d) % depth

    own = [
        pltpu.make_async_copy(class_in, class_ref, own_sem.at[0]),
        pltpu.make_async_copy(vol_ref.at[0], buf.at[me, pl.ds(0, rows)], own_sem.at[1]),
        pltpu.make_async_copy(defocus_in, defocus_ref, own_sem.at[2]),
        pltpu.make_async_copy(tilt_in, tilt_ref, own_sem.at[3]),
        pltpu.make_async_copy(table_ref.at[pl.ds(0, length), pl.ds(0, 2 * length)], fwd_ref, own_sem.at[4]),
    ]
    for copy in own:
        copy.start()
    barrier = pltpu.get_barrier_semaphore()
    for way, d in ((0, 1), (1, 1), (0, 2), (1, 2)):
        peer = at_distance(way, d) * 2 + core
        pl.semaphore_signal(barrier, inc=1, device_id={"batch": peer}, device_id_type=MESH)
    pl.semaphore_signal(barrier, inc=1, device_id={"batch": partner}, device_id_type=MESH)
    ids = lax.broadcasted_iota(jnp.int32, tally_buf.shape, 1)

    def count(p, tally):
        return tally + jnp.where(ids == class_ref[p], 1.0, 0.0)

    own[0].wait()
    tally = lax.fori_loop(0, total, count, jnp.zeros(ids.shape, jnp.float32), unroll=8)
    tally_buf[...] = tally.astype(jnp.bfloat16)
    own.append(pltpu.make_async_copy(tally_buf, buf.at[me, pl.ds(rows, tally_buf.shape[0])], own_sem.at[5]))
    own[-1].start()
    for copy in own[1:]:
        copy.wait()
    pl.semaphore_wait(barrier, 5)

    spans = (pl.ds(0, rows // 2), pl.ds(rows // 2, buf.shape[1] - rows // 2))

    def halves(way, d):
        return (0, 1) if d < far else (way,)

    def unit(way, d, h):
        return (way * far + d - 1) * 2 + h

    def ring(way, d, h, first):
        at = buf.at[at_distance(1 - way, first) * 2 + core, spans[h]]
        i = unit(way, d, h)
        return pltpu.make_async_remote_copy(
            src_ref=at, dst_ref=at, send_sem=ring_send.at[i], recv_sem=ring_recv.at[i],
            device_id={"batch": at_distance(way, d - first) * 2 + core}, device_id_type=MESH,
        )

    def arrival(way, d, h):
        at = buf.at[at_distance(1 - way, d) * 2 + core, spans[h]]
        i = unit(way, d, h)
        return pltpu.make_async_remote_copy(
            src_ref=at, dst_ref=at, send_sem=ring_send.at[i], recv_sem=ring_recv.at[i],
            device_id={"batch": at_distance(way, 1) * 2 + core}, device_id_type=MESH,
        )

    def pair(zz, i, h, which):
        at = buf.at[zz * 2 + which, spans[h]]
        return pltpu.make_async_remote_copy(
            src_ref=at, dst_ref=at, send_sem=pair_send.at[i], recv_sem=pair_recv.at[i],
            device_id={"batch": partner}, device_id_type=MESH,
        )

    sent = []
    own_unit = 4 * far

    def send(copy):
        copy.start()
        sent.append(copy)

    for d in (2, 1):
        for h in (0, 1):
            for way in (0, 1):
                send(ring(way, d, h, 0))
    for h in (0, 1):
        send(pair(z, own_unit + h, h, core))

    freq = lax.broadcasted_iota(jnp.int32, (8, length), 1)
    row = lax.broadcasted_iota(jnp.int32, (8, length), 0)
    signed = jnp.where(freq < length // 2, freq, freq - length)
    reach = (8 * jnp.abs(signed)).astype(jnp.float32)
    half = length // 2
    along_s = (signed * signed).astype(jnp.float32) * (0.5 / (half * half))
    lane_radius = 8 * (freq % 8) + row + 1
    along_r = (lane_radius * lane_radius).astype(jnp.float32) * (0.5 / (half * half))
    radii = [(row + (1 + r)).astype(jnp.float32) for r in range(0, period, 8)]
    phase = PHASE / (2.0 * math.pi)
    terms = sine_terms(7)

    def minus_sine(turns):
        u = turns - jnp.floor(turns + 0.5)
        w = u * u
        s = jnp.full_like(w, terms[-1])
        for c in terms[-2::-1]:
            s = s * w + c
        return s * u

    group = length // 8
    groups = total // group
    bounds = [q * groups // (far + 1) for q in range(far + 2)]
    a_copies = []

    def filters(q):
        first, last = bounds[q], bounds[q + 1]

        def body(b, carry):
            base = b * group
            ds = [defocus_ref[base + i] for i in range(group)]
            by_lane = jnp.full((8, length), ds[0], jnp.float32)
            for i in range(1, group):
                by_lane = jnp.where(freq >= 8 * i, ds[i], by_lane)
            turns_r = by_lane * along_r
            sine_r = minus_sine(turns_r)
            cosine_r = minus_sine(turns_r + 0.25)
            for e in range(0, group, 8):
                by_row = jnp.full((8, length), ds[e], jnp.float32)
                for i in range(1, 8):
                    by_row = jnp.where(row >= i, ds[e + i], by_row)
                turns_s = by_row * along_s + phase
                sine_s = minus_sine(turns_s)
                cosine_s = minus_sine(turns_s + 0.25)
                for i in range(8):
                    at = 8 * (e + i)
                    ss = jnp.broadcast_to(sine_s[i : i + 1, :], (8, length))
                    cs = jnp.broadcast_to(cosine_s[i : i + 1, :], (8, length))
                    tilt = tilt_ref[pl.ds(base + e + i, 1), :].astype(jnp.float32)
                    plus = jnp.broadcast_to(tilt[:, 0:1], (8, length))
                    limit = jnp.where(freq < length // 2, plus, jnp.broadcast_to(tilt[:, 1:2], (8, length)))
                    for n in range(period // 8):
                        sr = jnp.broadcast_to(sine_r[:, at + n : at + n + 1], (8, length))
                        cr = jnp.broadcast_to(cosine_r[:, at + n : at + n + 1], (8, length))
                        keep = reach <= limit * radii[n]
                        a_buf[base + e + i, 8 * n : 8 * n + 8, :] = jnp.where(keep, -(ss * cr + cs * sr), 0.0)
            return carry

        lax.fori_loop(first, last, body, 0)
        at = pl.ds(first * group, (last - first) * group)
        if last > first:
            a_copies.append(pltpu.make_async_copy(a_buf.at[at], a_out.at[at], a_sem.at[q]))
            a_copies[-1].start()

    v_copies = []

    def transform(slot, i):
        spectrum = jnp.dot(buf[slot, 0:rows, :], fwd_ref[0:length, :], preferred_element_type=jnp.float32)
        v_buf[slot] = spectrum.astype(jnp.bfloat16)
        copy = pltpu.make_async_copy(v_buf.at[slot], v_out.at[slot], v_sem.at[i])
        copy.start()
        v_copies.append(copy)

    def arrived(d):
        for h in (0, 1):
            for way in (0, 1):
                if h not in halves(way, d):
                    continue
                arrival(way, d, h).wait_recv()
                if d == 2:
                    send(ring(way, 3, h, 2))
                    if h in halves(way, far):
                        send(ring(way, far, h, 2))
        for h in (0, 1):
            for way in (0, 1):
                if h in halves(way, d):
                    send(pair(at_distance(1 - way, d), unit(way, d, h), h, core))

    def transforms(d):
        if d == 0:
            for h in (0, 1):
                pair(z, own_unit + h, h, other).wait_recv()
            transform(partner, len(v_copies))
            return
        for way in (0, 1) if d < far else (0,):
            transform(at_distance(1 - way, d) * 2 + core, len(v_copies))
        for way in (0, 1):
            for h in halves(way, d):
                pair(at_distance(1 - way, d), unit(way, d, h), h, other).wait_recv()
        for way in (0, 1) if d < far else (0,):
            transform(at_distance(1 - way, d) * 2 + other, len(v_copies))

    transform(me, 0)
    filters(0)
    arrived(2)
    filters(1)
    arrived(1)
    filters(2)
    transforms(0)
    transforms(2)
    transforms(1)
    arrived(3)
    filters(3)
    arrived(far)
    filters(4)
    transforms(3)
    transforms(far)
    tally = jnp.zeros((8, length), jnp.float32)
    for b in range(devices):
        tally += buf[b, rows : rows + 8, :].astype(jnp.float32)
    counts_out[...] = tally
    for copy in sent:
        copy.wait_send()
    for copy in v_copies + a_copies:
        copy.wait()


def gather_call(volumes, assignment, defocus, tilts, table, devices):
    _, rows, length = volumes.shape
    total = defocus.shape[0]
    period = length // 2
    assert devices == 16
    anywhere = pl.BlockSpec(memory_space=pl.ANY)
    inside = pl.BlockSpec(memory_space=pltpu.VMEM)
    sems = lambda n: pltpu.SemaphoreType.DMA((n,))
    return pl.pallas_call(
        gather_kernel,
        out_shape=(
            jax.ShapeDtypeStruct((devices, rows, 2 * length), jnp.bfloat16),
            jax.ShapeDtypeStruct((total, period, length), jnp.float32),
            jax.ShapeDtypeStruct((8, length), jnp.float32),
        ),
        in_specs=[pl.BlockSpec(memory_space=pltpu.HBM)] * 5,
        out_specs=(anywhere, anywhere, inside),
        scratch_shapes=[
            pltpu.VMEM((devices, rows + 16, length), jnp.bfloat16),
            pltpu.VMEM((devices, rows, 2 * length), jnp.bfloat16),
            pltpu.VMEM((total, period, length), jnp.float32),
            pltpu.VMEM((16, length), jnp.bfloat16),
            pltpu.VMEM((length, 2 * length), jnp.bfloat16),
            pltpu.VMEM(tilts.shape, jnp.int32),
            pltpu.SMEM((total,), jnp.float32),
            pltpu.SMEM((total,), jnp.int32),
            sems(6), sems(devices), sems(5),
            sems(devices), sems(devices), sems(devices + 2), sems(devices + 2),
        ],
        compiler_params=pltpu.CompilerParams(collective_id=0, has_side_effects=True, vmem_limit_bytes=16 << 20),
        name="gather",
    )(defocus, tilts, assignment, volumes, table)


def reduce_kernel(
    side, scale, g_ref, vol_ref, sc_ref, counts_ref, new_ref, scores_ref,
    from_pair, came, going, across, down,
    pair_send, pair_recv, ring_send, ring_recv, across_send, across_recv, down_send, down_recv,
):
    devices, rows, length = g_ref.shape
    depth = devices // 2
    far = depth // 2
    me = lax.axis_index("batch")
    z, core = me // 2, me % 2
    other = 1 - core
    partner = z * 2 + other
    c = lax.axis_index("cls")
    y, x = c // side, c % side
    in_row = [y * side + (x + d) % side for d in range(1, side)]
    in_column = [((y + d) % side) * side + x for d in range(1, side)]

    def at_distance(way, d):
        return (z + d) % depth if way == 0 else (z + depth - d) % depth

    barrier = pltpu.get_barrier_semaphore()
    for way, d in ((0, 1), (1, 1), (0, 2), (1, 2)):
        peer = at_distance(way, d) * 2 + core
        pl.semaphore_signal(barrier, inc=1, device_id={"batch": peer}, device_id_type=MESH)
    pl.semaphore_signal(barrier, inc=1, device_id={"batch": partner}, device_id_type=MESH)
    for peer in in_row + in_column:
        pl.semaphore_signal(barrier, inc=1, device_id={"cls": peer}, device_id_type=MESH)
    pl.semaphore_wait(barrier, 5 + 2 * (side - 1))

    order = [far]
    for d in range(far - 1, 0, -1):
        order += [d, depth - d]
    order.append(0)
    pairs = {}
    for i, d in enumerate(order):
        j = (z + d) % depth
        pairs[d] = pltpu.make_async_remote_copy(
            src_ref=g_ref.at[2 * j + other], dst_ref=from_pair.at[j],
            send_sem=pair_send.at[i], recv_sem=pair_recv.at[i],
            device_id={"batch": partner}, device_id_type=MESH,
        )
        pairs[d].start()

    def spread(ref, send, recv, peers, axis):
        copies = []
        for d, peer in enumerate(peers, 1):
            copies.append(pltpu.make_async_remote_copy(
                src_ref=ref.at[0], dst_ref=ref.at[d], send_sem=send.at[d - 1], recv_sem=recv.at[d - 1],
                device_id={axis: peer}, device_id_type=MESH,
            ))
            copies[-1].start()
        return copies

    across[0] = lax.dot_general(
        jnp.full((8, length), scale, jnp.float32), sc_ref[...], (((1,), (1,)), ((), ())),
        precision=lax.Precision.HIGHEST, preferred_element_type=jnp.float32,
    )
    row_copies = spread(across, across_send, across_recv, in_row, "cls")

    spans = (pl.ds(0, rows // 2), pl.ds(rows // 2, rows // 2))

    def mine(j, h):
        return g_ref[2 * j + core, spans[h], :].astype(jnp.float32) + from_pair[j, spans[h], :].astype(jnp.float32)

    def ring(way, d, h):
        i = (way * far + d - 1) * 2 + h
        return pltpu.make_async_remote_copy(
            src_ref=going.at[way, d - 1, spans[h]], dst_ref=came.at[way, d - 1, spans[h]],
            send_sem=ring_send.at[i], recv_sem=ring_recv.at[i],
            device_id={"batch": at_distance(way, d if d < 3 else d - 2) * 2 + core}, device_id_type=MESH,
        )

    sent = []

    def send(way, d, h, value):
        going[way, d - 1, spans[h], :] = value.astype(jnp.bfloat16)
        sent.append(ring(way, d, h))
        sent[-1].start()

    def landed(way, d, h):
        ring(way, d, h).wait_recv()
        return came[way, d - 1, spans[h], :].astype(jnp.float32)

    pairs[far].wait_recv()
    for way in (0, 1):
        send(way, far, way, mine(at_distance(way, far), way))
    for d in (3, 1):
        if d == 1:
            for copy in row_copies:
                copy.wait_recv()
            down[0] = sum(across[d] for d in range(1, side)) + across[0]
            column_copies = spread(down, down_send, down_recv, in_column, "cls")
        for way in (0, 1):
            pairs[d if way == 0 else depth - d].wait_recv()
            for h in (0, 1):
                send(way, d, h, mine(at_distance(way, d), h))
        if d == 3:
            for way in (0, 1):
                pairs[2 if way == 0 else depth - 2].wait_recv()
    for h in (0, 1):
        for way in (0, 1):
            value = mine(at_distance(way, 2), h) + landed(way, 3, h)
            if h == way:
                value += landed(way, far, h)
            send(way, 2, h, value)

    lane = lax.broadcasted_iota(jnp.int32, (1, length), 1)
    count = jnp.sum(jnp.where(lane == me, counts_ref[0:1, :], 0.0), axis=1, keepdims=True)
    factor = STEP / (count + 1.0)
    pairs[0].wait_recv()
    for h in (0, 1):
        value = mine(z, h)
        for d in (1, 2):
            for way in (0, 1):
                value += landed(way, d, h)
        new_ref[0, spans[h], :] = vol_ref[0, spans[h], :].astype(jnp.float32) + value * factor
    for copy in column_copies:
        copy.wait_recv()
    scores_ref[...] = sum(down[d] for d in range(1, side)) + down[0]
    for copy in sent + row_copies + column_copies + list(pairs.values()):
        copy.wait_send()


def reduce_call(g, volumes, partial, counts, scale, lanes):
    devices, rows, length = g.shape
    depth = devices // 2
    far = depth // 2
    side = math.isqrt(lanes)
    inside = pl.BlockSpec(memory_space=pltpu.VMEM)
    sems = lambda n: pltpu.SemaphoreType.DMA((n,))
    peers = max(side - 1, 1)
    return pl.pallas_call(
        functools.partial(reduce_kernel, side, scale),
        out_shape=(
            jax.ShapeDtypeStruct((1, rows, length), jnp.float32),
            jax.ShapeDtypeStruct((8, partial.shape[0]), jnp.float32),
        ),
        in_specs=[inside] * 4,
        out_specs=(inside, inside),
        scratch_shapes=[
            pltpu.VMEM((depth, rows, length), jnp.bfloat16),
            pltpu.VMEM((2, far, rows, length), jnp.bfloat16),
            pltpu.VMEM((2, far, rows, length), jnp.bfloat16),
            pltpu.VMEM((side, 8, partial.shape[0]), jnp.float32),
            pltpu.VMEM((side, 8, partial.shape[0]), jnp.float32),
            sems(depth), sems(depth), sems(4 * far), sems(4 * far),
            sems(peers), sems(peers), sems(peers), sems(peers),
        ],
        compiler_params=pltpu.CompilerParams(collective_id=1, has_side_effects=True, vmem_limit_bytes=12 << 20),
        name="reduce",
    )(g, volumes, partial, counts)


def main_kernel(
    x_ref, a_ref, spec_ref, table_ref, class_in, orient_in, g_ref, sc_ref,
    v_ref, acc_ref, fwd_ref, high_ref, low_ref, cls_ref, ori_ref, sem,
):
    step = pl.program_id(0)
    block, rows, length = x_ref.shape
    classes = spec_ref.shape[0]
    period = a_ref.shape[1]
    unit = length // ORIENTS

    @pl.when(step == 0)
    def _():
        copies = [
            pltpu.make_async_copy(table_ref.at[:, pl.ds(0, 2 * length)], fwd_ref, sem.at[0]),
            pltpu.make_async_copy(table_ref.at[:, pl.ds(2 * length, length)], high_ref, sem.at[1]),
            pltpu.make_async_copy(table_ref.at[:, pl.ds(3 * length, length)], low_ref, sem.at[2]),
            pltpu.make_async_copy(class_in, cls_ref, sem.at[3]),
            pltpu.make_async_copy(orient_in, ori_ref, sem.at[4]),
        ]
        for copy in copies:
            copy.start()

        @pl.loop(0, classes)
        def _(k):
            v_ref[k] = spec_ref[k].astype(jnp.float32)
            acc_ref[k] = jnp.zeros(acc_ref.shape[1:], jnp.float32)

        for copy in copies:
            copy.wait()

    for i in range(block):
        p = step * block + i
        k = cls_ref[p]
        start = pl.multiple_of(length - unit * ori_ref[p], unit)
        y = jnp.dot(x_ref[i], fwd_ref[pl.ds(start, length), :], preferred_element_type=jnp.float32)
        total = jnp.zeros((8, length), jnp.float32)
        for r in range(0, period, 8):
            a = a_ref[i, r : r + 8, :]
            for j in range(r, rows, period):
                for c in (0, length):
                    d = y[j : j + 8, c : c + length] - a * v_ref[k, j : j + 8, c : c + length]
                    total = total + d * d
                    acc_ref[k, j : j + 8, c : c + length] += a * d
        sc_ref[i, :] = jnp.sum(total, axis=0)

    @pl.when(step == pl.num_programs(0) - 1)
    def _():
        @pl.loop(0, classes)
        def _(k):
            s = acc_ref[k]
            s_high = s.astype(jnp.bfloat16)
            s_low = (s - s_high.astype(jnp.float32)).astype(jnp.bfloat16)
            g = jnp.dot(s_high, high_ref[...], preferred_element_type=jnp.float32)
            g += jnp.dot(s_low, high_ref[...], preferred_element_type=jnp.float32)
            g += jnp.dot(s_high, low_ref[...], preferred_element_type=jnp.float32)
            g_ref[k] = g.astype(jnp.bfloat16)


def main_call(x, a, spectra, assignment, orientation, table):
    total, rows, length = x.shape
    classes = spectra.shape[0]
    period = a.shape[1]
    outside = pl.BlockSpec(memory_space=pltpu.HBM)
    return pl.pallas_call(
        main_kernel,
        out_shape=(
            jax.ShapeDtypeStruct((classes, rows, length), jnp.bfloat16),
            jax.ShapeDtypeStruct((total, length), jnp.float32),
        ),
        grid=(total // BLOCK,),
        in_specs=[
            pl.BlockSpec((BLOCK, rows, length), lambda i: (i, 0, 0)),
            pl.BlockSpec((BLOCK, period, length), lambda i: (i, 0, 0)),
            pl.BlockSpec((classes, rows, 2 * length), lambda i: (0, 0, 0)),
            outside, outside, outside,
        ],
        out_specs=[
            pl.BlockSpec((classes, rows, length), lambda i: (0, 0, 0)),
            pl.BlockSpec((BLOCK, length), lambda i: (i, 0)),
        ],
        scratch_shapes=[
            pltpu.VMEM((classes, rows, 2 * length), jnp.float32),
            pltpu.VMEM((classes, rows, 2 * length), jnp.float32),
            pltpu.VMEM((2 * length, 2 * length), jnp.bfloat16),
            pltpu.VMEM((2 * length, length), jnp.bfloat16),
            pltpu.VMEM((2 * length, length), jnp.bfloat16),
            pltpu.SMEM((total,), jnp.int32),
            pltpu.SMEM((total,), jnp.int32),
            pltpu.SemaphoreType.DMA((5,)),
        ],
        compiler_params=pltpu.CompilerParams(vmem_limit_bytes=44 << 20),
        name="main",
    )(x, a, spectra, table, assignment, orientation)


def local(particles, volumes, assignment, defocus, tilt_limits, orientation):
    total, rows, length = particles.shape
    devices = lax.axis_size("batch")
    lanes = lax.axis_size("cls")
    assert volumes.shape[0] == 1 and rows % (length // 2) == 0
    table = tables(length)
    hbm = lambda v: pltpu.with_memory_space_constraint(v, pltpu.HBM)
    volumes, assignment, defocus, tilt_limits, table, orientation, particles = map(
        hbm, (volumes, assignment, defocus, tilt_limits, table, orientation, particles)
    )
    spectra, a, tally = gather_call(volumes, assignment, defocus, tilt_limits, table, devices)
    g, partial = main_call(particles, a, spectra, assignment, orientation, table)
    scale = 1.0 / (rows * lanes * length * length)
    updated, scores = reduce_call(g, volumes, partial, tally, scale, lanes)
    return updated, scores[0]


def solution(mesh):
    in_specs = (
        P("batch", "cls", None),
        P("batch", "cls", None),
        P("batch"),
        P("batch"),
        P("batch", None),
        P("batch"),
    )
    out_specs = (P("batch", "cls", None), P("batch"))
    return jax.shard_map(local, mesh=mesh, in_specs=in_specs, out_specs=out_specs, check_vma=False)
```

time: 80.1 us -> 69.2 us (0.86)
  local copies, waits for them, and re-layouts: 10.4 us -> 2.59 us
  Pallas kernels: 67.7 us -> 65.5 us
    unnamed x22 -> x2, local copies, waits for them, and re-layouts: 9.73 us -> 2.08 us
    pallas_call x1, Pallas kernels: 19.6 us -> 18.1 us  [reduce_call(): pl.pallas_call(functools.partial(reduce_kernel, side, scale), out_shape=(...]
where the time goes in v3:
time: 69.2 us; the launch traced here: 68.7 us
  Pallas kernels  65.5 us (95%)
  local copies, waits for them, and re-layouts  2.59 us (4%)
    pallas_call x1, Pallas kernels, gather_call(): pl.pallas_call(gather_kernel, out_shape=(jax.ShapeDtypeStruct((devices, r...  24.4 us
    pallas_call x1, Pallas kernels, main_call(): pl.pallas_call(main_kernel, out_shape=(jax.ShapeDtypeStruct((classes, row...  23 us
    pallas_call x1, Pallas kernels, reduce_call(): pl.pallas_call(functools.partial(reduce_kernel, side, scale), out_shape=(...  18.1 us
    unnamed x2, local copies, waits for them, and re-layouts  2.08 us

profile of v3, /device:TPU:1, one launch (start us, length us, event | category | flops | bytes accessed | tf_op | source)
XLA Modules:
  0.0 68.7 jit_solution(9402710792001536696)
XLA Ops:
  0.6 1.4 %copy.10.tilt_in = s32[128,2]{1,0:T(8,128)} copy(s32[128,2]{0,1:T(2,128)} %param.12) | data formatting | bytes 2048 | tf_op args[4]
  2.0 24.4 %gather.1 = (bf16[16,320,256]{2,1,0:T(8,128)(2,1)S(1)}, f32[128,64,128]{2,1,0:T(8,128)S(1)}, f32[8,128]{1,0:T(8,128)S(1)}) custom-call(f32[128]{0:T(128)} %defocus_in.1, s32[128,2]{1,0:T(8,128)} %copy.10.tilt_in, s32[128]{0:T(128)} %class_in.3, bf16[1,320,128]{2,1,0:T(8,128)(2,1)} %vol_ref.3, bf16[256,512]{1,0:T(8,128)(2,1)} %constant.12.table_ref), custom_call_target="tpu_custom_call" | custom-call | tf_op jit(solution)/shard_map/gather/pallas_call | solution.py:267
  26.4 23.0 %main.1 = (bf16[16,320,128]{2,1,0:T(8,128)(2,1)S(1)}, f32[128,128]{1,0:T(8,128)S(1)}) custom-call(bf16[128,320,128]{2,1,0:T(8,128)(2,1)} %x_ref.1, f32[128,64,128]{2,1,0:T(8,128)S(1)} %get-tuple-element.9.a_ref, bf16[16,320,256]{2,1,0:T(8,128)(2,1)S(1)} %get-tuple-element.10.spec_ref, bf16[256,512]{1,0:T(8,128)(2,1)} %constant.12.table_ref, s32[128]{0:T(128)} %class_in.3, ...), custom_call_target="tpu_custom_call" | custom-call | tf_op jit(solution)/shard_map/main/pallas_call | solution.py:509
  49.4 18.1 %reduce.1 = (f32[1,320,128]{2,1,0:T(8,128)S(1)}, f32[8,128]{1,0:T(8,128)S(1)}) custom-call(bf16[16,320,128]{2,1,0:T(8,128)(2,1)S(1)} %get-tuple-element.11.g_ref, bf16[1,320,128]{2,1,0:T(8,128)(2,1)} %vol_ref.3, f32[128,128]{1,0:T(8,128)S(1)} %get-tuple-element.12.sc_ref, f32[8,128]{1,0:T(8,128)S(1)} %get-tuple-element.13.counts_ref), custom_call_target="tpu_custom_call" | custom-call | tf_op jit(solution)/shard_map/reduce/pallas_call | solution.py:424
  67.5 0.5 slice_bitcast_fusion
  68.0 0.7 copy.12
